TPU v7x, 256 devices: a whole 4x4x8 slice. The times are simulated.
256 devices in a mesh: front: 16 (over z, core), grid: 16 (over x, y).
Axes of the slice: x: 4, y: 4, z: 8, core: 2. Of those that a mesh axis runs over, the one named last changes fastest.
Arguments:
- child_blocks: bfloat16 [32, 3072, 3072], P('grid', 'front'), may hold values from -1.5 to 6, as said below
- orig_diag: bfloat16 [16, 1024, 1024], P('front', None, 'grid'), may hold values from -2.5 to 81, as said below
- orig_rows: bfloat16 [16, 1024, 6144], P('front', None, 'grid'), may hold values from -1.5 to 1.5
- child_map: int32 [32, 24], replicated, may hold values from 0 to 55, as said below
- child_parent: int32 [32], replicated, may hold values from 0 to 15, as said below
- pivot_order: int32 [16, 56], replicated, may hold values from 0 to 55, as said below
Outputs:
- upper_diag: float32 [16, 1024, 1024], P('front', None, 'grid')
- upper_rows: float32 [16, 1024, 6144], P('front', None, 'grid')
- schur: bfloat16 [16, 6144, 6144], P('front', None, 'grid')
Inputs may be any that keep to these rules, and one draw needn't show every extreme that they name: `child_map`: each row names 24 different variable blocks. `child_parent`: every front is named by exactly two children. `pivot_order`: each row is a permutation of the front's variable blocks. `child_blocks`: each child's block is symmetric. `orig_diag`: each front's block is symmetric, and every pivot_block is positive definite.
All inputs are finite; a program needn't handle non-finite values.
Results may differ from a plain program's by a relative error of at most 0.001.
Values may be sent and summed in bfloat16 or wider, within the bound.
A program may use at most 128 MiB of HBM per device.

v0:
```python
import jax
import jax.numpy as jnp
from jax import lax
from jax.sharding import PartitionSpec as P

ORDER = 7168
PANEL = 1024
CHILD = 3072
BLOCK = 128


def child_order(child_parent):
    kid_total = child_parent.shape[0]
    kid_ids = jnp.arange(kid_total, dtype=jnp.int32)
    earlier = (child_parent[:, None] == child_parent[None, :]) & (
        kid_ids[None, :] < kid_ids[:, None]
    )
    kid_rank = jnp.sum(earlier.astype(jnp.int32), axis=1)
    kid_slot = 2 * child_parent + kid_rank
    matches = kid_slot[None, :] == kid_ids[:, None]
    return jnp.sum(jnp.where(matches, kid_ids[None, :], 0), axis=1)


def child_positions(parents, maps, pivot_order):
    front_total = pivot_order.shape[0]
    front_blocks = pivot_order.shape[1]
    chosen = (parents[:, None] == jnp.arange(front_total, dtype=jnp.int32)[None, :]).astype(
        jnp.int32
    )
    piv_rows = jnp.sum(chosen[:, :, None] * pivot_order[None, :, :], axis=1)
    slot_ids = jnp.arange(front_blocks, dtype=jnp.int32)
    matches = piv_rows[:, None, :] == maps[:, :, None]
    return jnp.sum(jnp.where(matches, slot_ids[None, None, :], 0), axis=2)


def shards(child_blocks, orig_diag, orig_rows, child_map, child_parent, pivot_order):
    groups = lax.axis_size("grid")
    front_total = lax.axis_size("front")
    grid_index = lax.axis_index("grid")
    front_index = lax.axis_index("front")
    kid_count = child_blocks.shape[0]
    slab_rows = child_blocks.shape[1]
    front_blocks = ORDER // BLOCK
    kid_blocks = CHILD // BLOCK
    panel_blocks = PANEL // BLOCK
    sub_rows = BLOCK // 2
    panel_cols = orig_diag.shape[2]
    trail_cols = orig_rows.shape[2]
    kid_order = child_order(child_parent)
    first_kid = grid_index * kid_count
    parents = lax.dynamic_slice_in_dim(child_parent, first_kid, kid_count, 0)
    maps = lax.dynamic_slice_in_dim(child_map, first_kid, kid_count, 0)
    landing = child_positions(parents, maps, pivot_order)
    spread = (
        landing[:, :, None] == jnp.arange(front_blocks, dtype=jnp.int32)[None, None, :]
    ).astype(jnp.bfloat16)
    tiles = child_blocks.reshape(kid_count, slab_rows, kid_blocks, BLOCK)
    panel_send = jnp.einsum(
        "krab,kap->krpb", tiles, spread[:, :, :panel_blocks], preferred_element_type=jnp.float32
    ).astype(jnp.bfloat16)
    panel_send = panel_send.reshape(kid_count, slab_rows, groups, panel_cols)
    trail_send = jnp.einsum(
        "krab,kap->krpb", tiles, spread[:, :, panel_blocks:], preferred_element_type=jnp.float32
    ).astype(jnp.bfloat16)
    trail_send = trail_send.reshape(kid_count, slab_rows, groups, trail_cols)
    panel_part = lax.all_to_all(panel_send, "grid", split_axis=2, concat_axis=0, tiled=True)
    trail_part = lax.all_to_all(trail_send, "grid", split_axis=2, concat_axis=0, tiled=True)
    row_count = panel_part.shape[1]
    panel_sorted = jnp.take(panel_part, kid_order, axis=0).reshape(
        front_total, 2, row_count, 1, panel_cols
    )
    trail_sorted = jnp.take(trail_part, kid_order, axis=0).reshape(
        front_total, 2, row_count, 1, trail_cols
    )
    panel_in = lax.all_to_all(panel_sorted, "front", split_axis=0, concat_axis=0, tiled=True)
    trail_in = lax.all_to_all(trail_sorted, "front", split_axis=0, concat_axis=0, tiled=True)
    own_kids = lax.dynamic_slice_in_dim(kid_order, 2 * front_index, 2, 0)
    chosen = (own_kids[:, None] == jnp.arange(2 * front_total, dtype=jnp.int32)[None, :]).astype(
        jnp.int32
    )
    own_maps = jnp.sum(chosen[:, :, None] * child_map[None, :, :], axis=1)
    own_parents = jnp.zeros((2,), jnp.int32) + front_index
    own_landing = child_positions(own_parents, own_maps, pivot_order)
    sub_land = (
        2 * jnp.repeat(own_landing, 2, axis=1)
        + jnp.tile(jnp.arange(2, dtype=jnp.int32), kid_blocks)[None, :]
    )
    row_spread = (
        sub_land[:, :, None] == jnp.arange(ORDER // sub_rows, dtype=jnp.int32)[None, None, :]
    ).astype(jnp.bfloat16)
    row_spread = row_spread.reshape(2, front_total, slab_rows // sub_rows, ORDER // sub_rows)
    panel_rows_in = panel_in.reshape(front_total, 2, slab_rows // sub_rows, sub_rows, panel_cols)
    trail_rows_in = trail_in.reshape(front_total, 2, slab_rows // sub_rows, sub_rows, trail_cols)
    diag_sum = jnp.einsum(
        "ftuxw,tfup->pxw",
        panel_rows_in,
        row_spread[:, :, :, : PANEL // sub_rows],
        preferred_element_type=jnp.float32,
    ).reshape(PANEL, panel_cols)
    trail_sum = jnp.einsum(
        "ftuxw,tfup->pxw", trail_rows_in, row_spread, preferred_element_type=jnp.float32
    ).reshape(ORDER, trail_cols)
    pivot_whole = lax.all_gather(
        diag_sum + orig_diag[0].astype(jnp.float32), "grid", axis=1, tiled=True
    )
    panel_rows = trail_sum[:PANEL] + orig_rows[0].astype(jnp.float32)
    trailing = trail_sum[PANEL:]
    lower_factor = jnp.linalg.cholesky(pivot_whole)
    pivots = jnp.diagonal(lower_factor)
    own_lower = lax.dynamic_slice_in_dim(lower_factor, grid_index * panel_cols, panel_cols, 0)
    upper_diag = pivots[:, None] * own_lower.T
    solved = jax.scipy.linalg.solve_triangular(lower_factor, panel_rows, lower=True)
    upper_rows = pivots[:, None] * solved
    rounded = solved.astype(jnp.bfloat16)
    contract_rows = (((0,), (0,)), ((), ()))
    schur = (
        trailing
        - lax.dot_general(
            lax.all_gather(rounded, "grid", axis=1, tiled=True),
            rounded,
            contract_rows,
            preferred_element_type=jnp.float32,
        )
    ).astype(jnp.bfloat16)
    return (upper_diag[None], upper_rows[None], schur[None])


def solution(mesh):
    return jax.shard_map(
        shards,
        mesh=mesh,
        in_specs=(
            P("grid", "front", None),
            P("front", None, "grid"),
            P("front", None, "grid"),
            P(),
            P(),
            P(),
        ),
        out_specs=(P("front", None, "grid"), P("front", None, "grid"), P("front", None, "grid")),
        check_vma=False,
    )
```

profile of v0, /device:TPU:2, one launch (start us, length us, event | category | flops | bytes accessed | tf_op | source)
XLA Modules:
  0.0 689.1 jit_solution(8000058685699687935)
XLA Ops:
  18.7 7.5 %all-to-all-start = ((bf16[2,192,16,64]{1,3,0,2:T(8,128)(2,1)}), bf16[2,192,16,64]{1,3,0,2:T(8,128)(2,1)S(1)}, u32[]{:S(2)}, u32[]{:S(2)}) async-start(bf16[2,192,16,64]{1,3,0,2:T(8,128)(2,1)} %copy.50), calls=%async_computation | async-start | bytes 2097152 | tf_op jit(solution)/shard_map/all_to_all | solution.py:66
  26.4 14.9 %all-to-all-done = bf16[2,192,16,64]{1,3,0,2:T(8,128)(2,1)S(1)} async-done(((bf16[2,192,16,64]{1,3,0,2:T(8,128)(2,1)}), bf16[2,192,16,64]{1,3,0,2:T(8,128)(2,1)S(1)}, u32[]{:S(2)}, u32[]{:S(2)}) %all-to-all-start) | async-done | bytes 786464 | tf_op jit(solution)/shard_map/all_to_all | solution.py:66
  45.2 8.6 %all-to-all-start.1 = ((bf16[16,2,192,1,64]{2,4,3,1,0:T(8,128)(2,1)}), bf16[16,2,192,1,64]{2,4,3,1,0:T(8,128)(2,1)S(1)}, u32[]{:S(2)}, u32[]{:S(2)}) async-start(bf16[16,2,192,1,64]{2,4,3,1,0:T(8,128)(2,1)} %broadcast_select_fusion), calls=%async_computation.1 | async-start | bytes 2097152 | tf_op jit(solution)/shard_map/all_to_all | solution.py:75
  55.5 24.8 %all-to-all-done.1 = bf16[16,2,192,1,64]{2,4,3,1,0:T(8,128)(2,1)S(1)} async-done(((bf16[16,2,192,1,64]{2,4,3,1,0:T(8,128)(2,1)}), bf16[16,2,192,1,64]{2,4,3,1,0:T(8,128)(2,1)S(1)}, u32[]{:S(2)}, u32[]{:S(2)}) %all-to-all-start.1) | async-done | bytes 786464 | tf_op jit(solution)/shard_map/all_to_all | solution.py:75
  81.9 3.2 copy.64
  87.9 3.6 convert_bitcast_fusion
  91.5 8.3 %reshape.373 = bf16[2,192,16,384]{3,2,1,0:T(8,128)(2,1)} reshape(bf16[2,192,48,128]{3,2,1,0:T(8,128)(2,1)} %convert_bitcast_fusion) | data formatting | bytes 9437184 | tf_op jit(solution)/shard_map/reshape | solution.py:65
  99.8 5.7 copy.56
  105.5 7.1 %all-to-all-start.2 = ((bf16[2,192,16,384]{3,1,0,2:T(8,128)(2,1)}), bf16[2,192,16,384]{3,1,0,2:T(8,128)(2,1)}, u32[]{:S(2)}, u32[]{:S(2)}) async-start(bf16[2,192,16,384]{3,1,0,2:T(8,128)(2,1)} %copy.56), calls=%async_computation.2 | async-start | bytes 9437184 | tf_op jit(solution)/shard_map/all_to_all | solution.py:67
  112.7 76.0 %all-to-all-done.2 = bf16[2,192,16,384]{3,1,0,2:T(8,128)(2,1)} async-done(((bf16[2,192,16,384]{3,1,0,2:T(8,128)(2,1)}), bf16[2,192,16,384]{3,1,0,2:T(8,128)(2,1)}, u32[]{:S(2)}, u32[]{:S(2)}) %all-to-all-start.2) | async-done | bytes 4718624 | tf_op jit(solution)/shard_map/all_to_all | solution.py:67
  188.6 5.9 gather_fusion.2
  194.5 5.1 select_bitcast_fusion
  199.6 5.8 all-to-all-start.3
  205.5 5.8 copy.54
  211.4 4.4 fusion.4
  217.8 11.7 %cholesky.223 = f32[128,128]{1,0:T(8,128)S(1)} custom-call(f32[128,128]{1,0:T(8,128)S(1)} %cholesky.580), custom_call_target="Cholesky" | custom-call | tf_op jit(solution)/shard_map/jit(cholesky)/cholesky | solution.py:108
  229.6 9.8 %custom-call.63 = f32[1,128,128]{1,2,0:T(8,128)S(1)} custom-call(f32[1,128,128]{2,1,0:T(8,128)S(1)} %get-tuple-element.63), custom_call_target="InvertDiagBlocksLowerTriangular" | custom-call | tf_op jit(solution)/shard_map/jit(cholesky)/cholesky | solution.py:108
  239.4 2.5 cholesky.255
  241.9 2.3 constant_dynamic-update-slice_fusion.25
  245.8 11.9 %cholesky.244 = f32[128,128]{1,0:T(8,128)S(1)} custom-call(f32[128,128]{1,0:T(8,128)S(1)} %cholesky.584), custom_call_target="Cholesky" | custom-call | tf_op jit(solution)/shard_map/jit(cholesky)/cholesky | solution.py:108
  258.4 9.8 %custom-call.64 = f32[1,128,128]{1,2,0:T(8,128)S(1)} custom-call(f32[1,128,128]{2,1,0:T(8,128)S(1)} %get-tuple-element.60), custom_call_target="InvertDiagBlocksLowerTriangular" | custom-call | tf_op jit(solution)/shard_map/jit(cholesky)/cholesky | solution.py:108
  271.5 11.7 %cholesky.468 = f32[128,128]{1,0:T(8,128)S(1)} custom-call(f32[128,128]{1,0:T(8,128)S(1)} %cholesky.589), custom_call_target="Cholesky" | custom-call | tf_op jit(solution)/shard_map/jit(cholesky)/cholesky | solution.py:108
  283.9 9.8 %custom-call.65 = f32[1,128,128]{1,2,0:T(8,128)S(1)} custom-call(f32[1,128,128]{2,1,0:T(8,128)S(1)} %get-tuple-element.57), custom_call_target="InvertDiagBlocksLowerTriangular" | custom-call | tf_op jit(solution)/shard_map/jit(cholesky)/cholesky | solution.py:108
  294.9 2.3 convolution_subtract_fusion.2
  297.2 11.9 %cholesky.487 = f32[128,128]{1,0:T(8,128)S(1)} custom-call(f32[128,128]{1,0:T(8,128)S(1)} %cholesky.594), custom_call_target="Cholesky" | custom-call | tf_op jit(solution)/shard_map/jit(cholesky)/cholesky | solution.py:108
  309.8 9.8 %custom-call.66 = f32[1,128,128]{1,2,0:T(8,128)S(1)} custom-call(f32[1,128,128]{2,1,0:T(8,128)S(1)} %get-tuple-element.54), custom_call_target="InvertDiagBlocksLowerTriangular" | custom-call | tf_op jit(solution)/shard_map/jit(cholesky)/cholesky | solution.py:108
  320.7 2.3 convolution_subtract_fusion.3
  323.1 11.7 %cholesky.506 = f32[128,128]{1,0:T(8,128)S(1)} custom-call(f32[128,128]{1,0:T(8,128)S(1)} %cholesky.599), custom_call_target="Cholesky" | custom-call | tf_op jit(solution)/shard_map/jit(cholesky)/cholesky | solution.py:108
  335.4 10.2 %custom-call.67 = f32[1,128,128]{1,2,0:T(8,128)S(1)} custom-call(f32[1,128,128]{2,1,0:T(8,128)S(1)} %get-tuple-element.51), custom_call_target="InvertDiagBlocksLowerTriangular" | custom-call | tf_op jit(solution)/shard_map/jit(cholesky)/cholesky | solution.py:108
  348.9 11.7 %cholesky.526 = f32[128,128]{1,0:T(8,128)S(1)} custom-call(f32[128,128]{1,0:T(8,128)S(1)} %cholesky.604), custom_call_target="Cholesky" | custom-call | tf_op jit(solution)/shard_map/jit(cholesky)/cholesky | solution.py:108
  361.3 9.8 %custom-call.68 = f32[1,128,128]{1,2,0:T(8,128)S(1)} custom-call(f32[1,128,128]{2,1,0:T(8,128)S(1)} %get-tuple-element.48), custom_call_target="InvertDiagBlocksLowerTriangular" | custom-call | tf_op jit(solution)/shard_map/jit(cholesky)/cholesky | solution.py:108
  374.1 11.7 %cholesky.546 = f32[128,128]{1,0:T(8,128)S(1)} custom-call(f32[128,128]{1,0:T(8,128)S(1)} %cholesky.609), custom_call_target="Cholesky" | custom-call | tf_op jit(solution)/shard_map/jit(cholesky)/cholesky | solution.py:108
  386.4 9.8 %custom-call.69 = f32[1,128,128]{1,2,0:T(8,128)S(1)} custom-call(f32[1,128,128]{2,1,0:T(8,128)S(1)} %get-tuple-element.45), custom_call_target="InvertDiagBlocksLowerTriangular" | custom-call | tf_op jit(solution)/shard_map/jit(cholesky)/cholesky | solution.py:108
  398.9 11.7 %cholesky.564 = f32[128,128]{1,0:T(8,128)S(1)} custom-call(f32[128,128]{1,0:T(8,128)S(1)} %convolution_subtract_fusion.13), custom_call_target="Cholesky" | custom-call | tf_op jit(solution)/shard_map/jit(cholesky)/cholesky | solution.py:108
  421.6 6.7 fusion.5
  428.3 23.2 %while.1 = (s32[]{:T(128)}, f32[1024,1024]{1,0:T(8,128)}, s32[8,2]{0,1:T(2,128)S(1)}, f32[8,128,128]{2,1,0:T(8,128)S(1)}, s32[]{:T(128)}) while((s32[]{:T(128)}, f32[1024,1024]{1,0:T(8,128)}, s32[8,2]{0,1:T(2,128)S(1)}, f32[8,128,128]{2,1,0:T(8,128)S(1)}, s32[]{:T(128)}) %tuple.61), condition=%wide.while_cond, body=%wide.while_body.sunk | while | flops 2 | bytes 131189 | solution.py:112
  428.9 2.3 bitcast_dynamic-update-slice_fusion.10
  431.9 2.3 bitcast_dynamic-update-slice_fusion.10
  434.8 2.3 bitcast_dynamic-update-slice_fusion.10
  437.7 2.3 bitcast_dynamic-update-slice_fusion.10
  440.6 2.3 bitcast_dynamic-update-slice_fusion.10
  451.5 78.6 %custom-call.70 = f32[8,128,128]{1,2,0:T(8,128)S(1)} custom-call(f32[8,128,128]{2,1,0:T(8,128)S(1)} %get-tuple-element.10), custom_call_target="InvertDiagBlocksLowerTriangular" | custom-call | tf_op jit(solution)/shard_map/jit(_solve_triangular)/triangular_solve | solution.py:112
  530.2 7.2 %fusion.6 = f32[112,64,384]{2,0,1:T(8,128)S(1)} fusion(bf16[16,2,3,64,384]{4,3,2,1,0:T(8,128)(2,1)} %bitcast.42, s32[2,16,3]{1,2,0:T(4,128)S(1)} %copy-done.10), kind=kOutput, calls=%fused_computation.17 | convolution fusion | flops 528493056 | bytes 15729024 | tf_op jit(solution)/shard_map/ftuxw,tfup->pxw/dot_general | solution.py:100
  555.2 17.4 %gather_fusion.1 = f32[1024]{0:T(1024)S(1)} fusion(f32[1024,1024]{1,0:T(8,128)} %get-tuple-element.22, s32[1024]{0:T(1024)S(1)} %bitcast.214), kind=kCustom, calls=%fused_computation.1 | custom fusion | bytes 16384 | tf_op jit(solution)/shard_map/jit(diagonal)/cond/branch_0_fun/gather | solution.py:109
  574.2 3.7 slice-done
  577.9 9.0 %copy.61 = f32[96,64,384]{2,1,0:T(8,128)} copy(f32[96,64,384]{2,0,1:T(8,128)S(1)} %slice-done) | data formatting | bytes 18874368 | tf_op jit(solution)/shard_map/slice | solution.py:107
  588.3 80.9 %all-gather.5.cloned.1.call-done = bf16[1024,6144]{1,0:T(8,128)(2,1)} async-done(((bf16[1024,384]{1,0:T(8,128)(2,1)}), bf16[1024,6144]{1,0:T(8,128)(2,1)}) %all-gather.5.cloned.1.call-update) | async-done | bytes 12582928 | tf_op jit(solution)/shard_map/all_gather | solution.py:119
  669.2 12.6 %fusion.1 = bf16[1,6144,384]{2,1,0:T(8,128)(2,1)} fusion(bf16[1024,6144]{1,0:T(8,128)(2,1)} %all-gather.5.cloned.1.call-done, bf16[1024,384]{1,0:T(8,128)(2,1)S(1)} %copy-done.4, f32[96,64,384]{2,1,0:T(8,128)} %copy.61), kind=kOutput, calls=%fused_computation.7 | convolution fusion | flops 4836556800 | bytes 27525120 | tf_op jit(solution)/shard_map/dot_general | solution.py:118
  (159 shorter events, 81.7 us)
Async XLA Ops:
  18.7 22.5 %all-to-all-start = ((bf16[2,192,16,64]{1,3,0,2:T(8,128)(2,1)}), bf16[2,192,16,64]{1,3,0,2:T(8,128)(2,1)S(1)}, u32[]{:S(2)}, u32[]{:S(2)}) async-start(bf16[2,192,16,64]{1,3,0,2:T(8,128)(2,1)} %copy.50), calls=%async_computation | async-start | bytes 2097152 | tf_op jit(solution)/shard_map/all_to_all | solution.py:66
  26.3 27.6 %copy-start.11 = (s32[1024]{0:T(1024)}, s32[1024]{0:T(1024)S(1)}, u32[]{:S(2)}) copy-start(s32[1024]{0:T(1024)S(1)} %pad_clamp_fusion) | copy-start | bytes 12292
  26.3 27.5 %copy-start.7 = (pred[16,2]{1,0:T(8,128)(4,1)}, pred[16,2]{1,0:T(8,128)(4,1)S(1)}, u32[]{:S(2)}) copy-start(pred[16,2]{1,0:T(8,128)(4,1)S(1)} %compare_and_fusion) | copy-start | bytes 100
  41.3 1.0 copy-start.2
  45.2 35.1 %all-to-all-start.1 = ((bf16[16,2,192,1,64]{2,4,3,1,0:T(8,128)(2,1)}), bf16[16,2,192,1,64]{2,4,3,1,0:T(8,128)(2,1)S(1)}, u32[]{:S(2)}, u32[]{:S(2)}) async-start(bf16[16,2,192,1,64]{2,4,3,1,0:T(8,128)(2,1)} %broadcast_select_fusion), calls=%async_computation.1 | async-start | bytes 2097152 | tf_op jit(solution)/shard_map/all_to_all | solution.py:75
  53.8 151.7 %all-gather.3.cloned.1.call-start = ((), (), s32[]{:S(2)}) async-start(), calls=%async_computation.4 | async-start | bytes 4456448 | tf_op jit(solution)/shard_map/all_gather | solution.py:103
  54.2 0.6 copy-start.9
  55.5 31.7 %copy-start.6 = (bf16[1,1024,64]{1,2,0:T(8,128)(2,1)S(1)}, bf16[1,1024,64]{1,2,0:T(8,128)(2,1)}, u32[]{:S(2)}) copy-start(bf16[1,1024,64]{1,2,0:T(8,128)(2,1)} %param.7) | copy-start | bytes 393220
  105.5 83.1 %all-to-all-start.2 = ((bf16[2,192,16,384]{3,1,0,2:T(8,128)(2,1)}), bf16[2,192,16,384]{3,1,0,2:T(8,128)(2,1)}, u32[]{:S(2)}, u32[]{:S(2)}) async-start(bf16[2,192,16,384]{3,1,0,2:T(8,128)(2,1)} %copy.56), calls=%async_computation.2 | async-start | bytes 9437184 | tf_op jit(solution)/shard_map/all_to_all | solution.py:67
  188.6 5.9 copy-start.8
  199.6 330.5 %all-to-all-start.3 = ((bf16[16,2,192,1,384]{4,2,1,3,0:T(8,128)(2,1)}), bf16[16,2,192,1,384]{4,2,1,3,0:T(8,128)(2,1)}, u32[]{:S(2)}, u32[]{:S(2)}) async-start(bf16[16,2,192,1,384]{4,2,1,3,0:T(8,128)(2,1)} %select_bitcast_fusion), calls=%async_computation.3 | async-start | bytes 9437184 | tf_op jit(solution)/shard_map/all_to_all | solution.py:76
  205.5 463.8 %all-gather.5.cloned.1.call-start = ((), (), s32[]{:S(2)}) async-start(), calls=%async_computation.5 | async-start | bytes 13369344 | tf_op jit(solution)/shard_map/all_gather | solution.py:119
  215.8 2.0 copy-start.1
  421.6 108.6 %copy-start.10 = (s32[2,16,3]{1,2,0:T(4,128)S(1)}, s32[2,16,3]{1,2,0:T(4,128)}, u32[]{:S(2)}) copy-start(s32[2,16,3]{1,2,0:T(4,128)} %copy-done.9) | copy-start | bytes 1156
  537.4 12.0 %copy-start = (f32[112,64,384]{2,0,1:T(8,128)}, f32[112,64,384]{2,0,1:T(8,128)S(1)}, u32[]{:S(2)}) copy-start(f32[112,64,384]{2,0,1:T(8,128)S(1)} %fusion.6) | copy-start | bytes 33030148
  537.4 1.7 copy-start.5
  554.3 0.9 copy-start.3
  574.2 3.7 slice-start
  577.9 91.3 %copy-start.4 = (bf16[1024,384]{1,0:T(8,128)(2,1)S(1)}, bf16[1024,384]{1,0:T(8,128)(2,1)}, u32[]{:S(2)}) copy-start(bf16[1024,384]{1,0:T(8,128)(2,1)} %copy-done.3) | copy-start | bytes 2359300
Sparse Core Ops, SparseCore 0:
  88.0 102.8 all-gather.2
  555.3 113.8 all-gather.4
where the time goes:
time: 698 us; the launch traced here: 689 us
  other arithmetic  277 us (40%)
  waiting for transfers between devices  197 us (28%)
  local copies, waits for them, and re-layouts  101 us (14%)
  matrix products  64.2 us (9%)
  starting transfers between devices  29.1 us (4%)
  between operations  20.4 us (3%)
    another operation x31, other arithmetic, shards(): lower_factor = jnp.linalg.cholesky(pivot_whole)  173 us
    another operation x3, other arithmetic, shards(): jax.scipy.linalg.solve_triangular(lower_factor, panel_rows, lower=True)  85.3 us
    all_gather x1, waiting for transfers between devices, shards(): lax.all_gather(rounded, 'grid', axis=1, tiled=True)  80.9 us
    all_to_all x1, waiting for transfers between devices, shards(): lax.all_to_all(trail_send, 'grid', split_axis=2, concat_axis=0, tiled=True)  76 us
    all_to_all x1, waiting for transfers between devices, shards(): lax.all_to_all(panel_sorted, 'front', split_axis=0, concat_axis=0, tiled=...  24.8 us
    another operation x14, matrix products, shards(): lower_factor = jnp.linalg.cholesky(pivot_whole)  23.1 us
    another operation x24, local copies, waits for them, and re-layouts  23 us
    gather x1, local copies, waits for them, and re-layouts, shards(): pivots = jnp.diagonal(lower_factor)  17.4 us
  transfers between devices with their start and end apart: 6, of which 4 were waited for; matrix products, arithmetic and copies ran while one was open for 55% of the time, Pallas kernels for 0%

commit v1 on v0

--- a/solution.py
+++ b/solution.py
@@ -1,12 +1,107 @@
 import jax
 import jax.numpy as jnp
 from jax import lax
+from jax.experimental import pallas as pl
+from jax.experimental.pallas import tpu as pltpu
 from jax.sharding import PartitionSpec as P
 
 ORDER = 7168
 PANEL = 1024
 CHILD = 3072
 BLOCK = 128
+N = 1024
+NB = 128
+PC = 384
+WT = N + PC
+F32 = jnp.float32
+BF = jnp.bfloat16
+
+
+def split(x):
+    hi=x.astype(BF); return hi,(x-hi.astype(F32)).astype(BF)
+def dg(a,b,ca,cb):
+    return lax.dot_general(a,b,(((ca,),(cb,)),((),())),preferred_element_type=F32)
+def factor_block(m_ref, inv_ref):
+    rid = lax.broadcasted_iota(jnp.int32,(8,1),0)
+    G=[m_ref[8*g:8*g+8,:] for g in range(16)]
+    B=lambda x:jnp.broadcast_to(x,(8,128))
+    for q in range(16):
+        c0=8*q
+        Rb=[jnp.broadcast_to(G[q][s:s+1,:],(8,256)) for s in range(8)]
+        E=[[B(Rb[s][:,c0+t:c0+t+1]) if t>=s else None for t in range(8)] for s in range(8)]
+        inv=[None]*8
+        for t in range(8):
+            inv[t]=1.0/E[t][t]
+            for s in range(t+1,8):
+                m=E[t][s]*inv[t]
+                for u in range(s,8): E[s][u]=E[s][u]-m*E[t][u]
+                Rb[s]=Rb[s]-jnp.concatenate([m,m],1)*Rb[t]
+        new=Rb[7]; iv=inv[7]
+        for s in range(6,-1,-1):
+            new=jnp.where(rid==s,Rb[s],new); iv=jnp.where(rid==s,inv[s],iv)
+        m_ref[c0:c0+8,:]=new
+        inv_ref[c0:c0+8,:]=iv
+        if q<15:
+            T=jnp.transpose(new[:,:128]*iv)
+            for g in range(q+1,16):
+                p=[T[8*g:8*g+8,t:t+1]*Rb[t] for t in range(8)]
+                G[g]=G[g]-(((p[0]+p[1])+(p[2]+p[3]))+((p[4]+p[5])+(p[6]+p[7])))
+def lu_kernel(a_ref,p_ref,ud_ref,ur_ref,s_ref,w,m_ref,inv_ref,uh,ul):
+    g=lax.axis_index("grid")
+    w[:,:N]=a_ref[...]; w[:,N:]=p_ref[...]
+    eye=(lax.broadcasted_iota(jnp.int32,(NB,NB),0)==lax.broadcasted_iota(jnp.int32,(NB,NB),1)).astype(F32)
+    def step(k,c):
+        r0=pl.multiple_of(k*NB,NB)
+        m_ref[:,:NB]=w[pl.ds(r0,NB),pl.ds(r0,NB)]
+        m_ref[:,NB:]=eye
+        factor_block(m_ref,inv_ref)
+        lh,ll=split(m_ref[:,NB:])
+        ah,al=split(w[pl.ds(r0,NB),:])
+        u=dg(lh,ah,1,0)+(dg(lh,al,1,0)+dg(ll,ah,1,0))
+        w[pl.ds(r0,NB),:]=u
+        h,l=split(u); uh[...]=h; ul[...]=l
+        iv=inv_ref[...]
+        x=u[:,N:]
+        ur_ref[pl.ds(r0,NB),:]=x
+        rs=jnp.sqrt(iv)
+        s_ref[pl.ds(r0,NB),:]=(x*jnp.concatenate([rs]*3,1)).astype(BF)
+        def upd(i,c):
+            i0=pl.multiple_of(i*NB,NB)
+            xh,xl=split((uh[:,pl.ds(i0,NB)].astype(F32)+ul[:,pl.ds(i0,NB)].astype(F32))*iv)
+            d=dg(xh,uh[...],0,0)+(dg(xh,ul[...],0,0)+dg(xl,uh[...],0,0))
+            w[pl.ds(i0,NB),:]=w[pl.ds(i0,NB),:]-d
+            return c
+        lax.fori_loop(k+1,N//NB,upd,0)
+        return c
+    lax.fori_loop(0,N//NB,step,0)
+    blk=pl.multiple_of((g//2)*NB,NB)
+    x=w[:,pl.ds(blk,NB)]
+    half=g%2
+    x=jnp.where(half==1,x[:,64:],x[:,:64])
+    col=64*g+lax.broadcasted_iota(jnp.int32,(N,64),1)
+    ud_ref[...]=jnp.where(lax.broadcasted_iota(jnp.int32,(N,64),0)<=col,x,0.0)
+
+
+def lu_call(a, p):
+    vm = pl.BlockSpec(memory_space=pltpu.VMEM)
+    return pl.pallas_call(
+        lu_kernel,
+        out_shape=(
+            jax.ShapeDtypeStruct((N, 64), F32),
+            jax.ShapeDtypeStruct((N, PC), F32),
+            jax.ShapeDtypeStruct((N, PC), BF),
+        ),
+        in_specs=[vm, vm],
+        out_specs=(vm, vm, vm),
+        scratch_shapes=[
+            pltpu.VMEM((N, WT), F32),
+            pltpu.VMEM((NB, 2 * NB), F32),
+            pltpu.VMEM((NB, NB), F32),
+            pltpu.VMEM((NB, WT), BF),
+            pltpu.VMEM((NB, WT), BF),
+        ],
+        compiler_params=pltpu.CompilerParams(vmem_limit_bytes=48 << 20),
+    )(a, p)
 
 
 def child_order(child_parent):
@@ -105,13 +200,7 @@
     )
     panel_rows = trail_sum[:PANEL] + orig_rows[0].astype(jnp.float32)
     trailing = trail_sum[PANEL:]
-    lower_factor = jnp.linalg.cholesky(pivot_whole)
-    pivots = jnp.diagonal(lower_factor)
-    own_lower = lax.dynamic_slice_in_dim(lower_factor, grid_index * panel_cols, panel_cols, 0)
-    upper_diag = pivots[:, None] * own_lower.T
-    solved = jax.scipy.linalg.solve_triangular(lower_factor, panel_rows, lower=True)
-    upper_rows = pivots[:, None] * solved
-    rounded = solved.astype(jnp.bfloat16)
+    upper_diag, upper_rows, rounded = lu_call(pivot_whole, panel_rows)
     contract_rows = (((0,), (0,)), ((), ()))
     schur = (
         trailing

time: 698 us -> 469 us (0.67); the launches traced: 689 us -> 468 us
  other arithmetic: 277 us -> 10.9 us
  waiting for transfers between devices: 197 us -> 269 us
  Pallas kernels: 0 us -> 67.3 us
  local copies, waits for them, and re-layouts: 101 us -> 52.7 us
  matrix products: 64.2 us -> 25.1 us
    another operation x34 -> x0, other arithmetic: 258 us -> none  [the longest x31 173 us: shards(): lower_factor = jnp.linalg.cholesky(pivot_whole)]
    all_gather x1, waiting for transfers between devices: 0.02 us -> 68.1 us  [shards(): lax.all_gather(diag_sum + orig_diag[0].astype(jnp.float32), 'grid', axis=...]
    pallas_call x0 -> x1, Pallas kernels: none -> 67.3 us  [lu_call(): pl.pallas_call(lu_kernel, out_shape=(jax.ShapeDtypeStruct((N, 64), F32),...]
    another operation x29 -> x0, matrix products: 37.5 us -> none  [the longest x14 23.1 us: shards(): lower_factor = jnp.linalg.cholesky(pivot_whole)]
    all_to_all x1, waiting for transfers between devices: 0.01 us -> 27.5 us  [shards(): lax.all_to_all(trail_sorted, 'front', split_axis=0, concat_axis=0, tiled=...]
    another operation x35 -> x0, local copies, waits for them, and re-layouts: 25.7 us -> none
    all_gather x1, waiting for transfers between devices: 80.9 us -> 99.2 us  [shards(): lax.all_gather(rounded, 'grid', axis=1, tiled=True)]
    gather x1 -> x0, local copies, waits for them, and re-layouts: 17.4 us -> none  [shards(): pivots = jnp.diagonal(lower_factor)]
  transfers between devices with their start and end apart: 6 -> 6, of which waited for: 4 -> 5; matrix products, arithmetic and copies ran while one was open for 55% -> 11% of each run, Pallas kernels for 0% -> 0%
where the time goes in v1:
time: 469 us; the launch traced here: 468 us
  waiting for transfers between devices  269 us (57%)
  Pallas kernels  67.3 us (14%)
  local copies, waits for them, and re-layouts  52.7 us (11%)
  starting transfers between devices  28.5 us (6%)
  matrix products  25.1 us (5%)
  between operations  14.2 us (3%)
  other arithmetic  10.9 us (2%)
    all_gather x1, waiting for transfers between devices, shards(): lax.all_gather(rounded, 'grid', axis=1, tiled=True)  99.2 us
    all_gather x1, waiting for transfers between devices, shards(): lax.all_gather(diag_sum + orig_diag[0].astype(jnp.float32), 'grid', axis=...  68.1 us
    pallas_call x1, Pallas kernels, lu_call(): pl.pallas_call(lu_kernel, out_shape=(jax.ShapeDtypeStruct((N, 64), F32),...  67.3 us
    all_to_all x1, waiting for transfers between devices, shards(): lax.all_to_all(trail_send, 'grid', split_axis=2, concat_axis=0, tiled=True)  59 us
    all_to_all x1, waiting for transfers between devices, shards(): lax.all_to_all(trail_sorted, 'front', split_axis=0, concat_axis=0, tiled=...  27.5 us
    all_to_all x1, waiting for transfers between devices, shards(): lax.all_to_all(panel_sorted, 'front', split_axis=0, concat_axis=0, tiled=...  15.6 us
    reshape x2, local copies, waits for them, and re-layouts, shards(): trail_send = trail_send.reshape(kid_count, slab_rows, groups, trail_cols)  14 us
    slice x3, local copies, waits for them, and re-layouts, shards(): trailing = trail_sum[PANEL:]  12.7 us
  transfers between devices with their start and end apart: 6, of which 5 were waited for; matrix products, arithmetic and copies ran while one was open for 11% of the time, Pallas kernels for 0%

profile of v1, /device:TPU:2, one launch (start us, length us, event | category | flops | bytes accessed | tf_op | source)
XLA Modules:
  0.0 468.2 jit_solution(7331951496944533695)
XLA Ops:
  7.2 0.9 convert_reduce_fusion
  8.1 0.7 dynamic_slice.10
  8.9 0.7 multiply_add_fusion
  9.6 0.1 select_reduce_fusion.2
  9.8 0.8 constant_dynamic-slice_fusion
  10.6 0.8 multiply_reduce_fusion
  11.4 0.1 copy.68
  11.5 0.8 multiply_reduce_fusion.2
  12.3 0.2 select_reduce_fusion
  12.5 2.2 copy.96
  14.8 1.4 fusion.13
  16.2 1.5 copy.69
  17.7 1.0 copy.70
  18.7 7.5 %all-to-all-start = ((bf16[2,192,16,64]{1,3,0,2:T(8,128)(2,1)}), bf16[2,192,16,64]{1,3,0,2:T(8,128)(2,1)S(1)}, u32[]{:S(2)}, u32[]{:S(2)}) async-start(bf16[2,192,16,64]{1,3,0,2:T(8,128)(2,1)} %copy.70), calls=%async_computation | async-start | bytes 2097152 | tf_op jit(solution)/shard_map/all_to_all | solution.py:161
  26.2 3.5 convert_bitcast_fusion
  29.8 8.3 %reshape.174 = bf16[2,192,16,384]{3,2,1,0:T(8,128)(2,1)} reshape(bf16[2,192,48,128]{3,2,1,0:T(8,128)(2,1)} %convert_bitcast_fusion) | data formatting | bytes 9437184 | tf_op jit(solution)/shard_map/reshape | solution.py:160
  38.1 5.7 %copy.75 = bf16[2,192,16,384]{3,1,0,2:T(8,128)(2,1)} copy(bf16[2,192,16,384]{3,2,1,0:T(8,128)(2,1)} %reshape.174) | data formatting | bytes 9437184 | tf_op jit(solution)/shard_map/reshape | solution.py:160
  43.8 7.2 %all-to-all-start.2 = ((bf16[2,192,16,384]{3,1,0,2:T(8,128)(2,1)}), bf16[2,192,16,384]{3,1,0,2:T(8,128)(2,1)}, u32[]{:S(2)}, u32[]{:S(2)}) async-start(bf16[2,192,16,384]{3,1,0,2:T(8,128)(2,1)} %copy.75), calls=%async_computation.2 | async-start | bytes 9437184 | tf_op jit(solution)/shard_map/all_to_all | solution.py:162
  51.0 0.1 reduce_sum.72
  51.2 0.6 gather_fusion
  51.8 1.1 broadcast_select_fusion
  52.9 59.0 %all-to-all-done.2 = bf16[2,192,16,384]{3,1,0,2:T(8,128)(2,1)} async-done(((bf16[2,192,16,384]{3,1,0,2:T(8,128)(2,1)}), bf16[2,192,16,384]{3,1,0,2:T(8,128)(2,1)}, u32[]{:S(2)}, u32[]{:S(2)}) %all-to-all-start.2) | async-done | bytes 4718624 | tf_op jit(solution)/shard_map/all_to_all | solution.py:162
  111.9 8.6 %all-to-all-start.1 = ((bf16[16,2,192,1,64]{2,4,3,1,0:T(8,128)(2,1)}), bf16[16,2,192,1,64]{2,4,3,1,0:T(8,128)(2,1)S(1)}, u32[]{:S(2)}, u32[]{:S(2)}) async-start(bf16[16,2,192,1,64]{2,4,3,1,0:T(8,128)(2,1)} %broadcast_select_fusion), calls=%async_computation.1 | async-start | bytes 2097152 | tf_op jit(solution)/shard_map/all_to_all | solution.py:170
  120.5 5.7 %gather_fusion.1 = bf16[32,192,384]{2,1,0:T(8,128)(2,1)} fusion(bf16[32,192,384]{2,1,0:T(8,128)(2,1)} %bitcast.20, s32[1024]{0:T(1024)S(1)} %pad_clamp_fusion), kind=kCustom, calls=%fused_computation.1 | custom fusion | bytes 9437312 | tf_op jit(solution)/shard_map/jit(_take)/gather | solution.py:167
  126.2 5.1 %select_bitcast_fusion = bf16[16,2,192,1,384]{4,2,1,3,0:T(8,128)(2,1)} fusion(bf16[16,2,192,1,384]{4,2,1,0,3:T(8,128)(2,1)} %bitcast.95, pred[16,2]{1,0:T(8,128)(4,1)S(1)} %compare_and_fusion), kind=kLoop, calls=%fused_computation.7 | loop fusion | flops 2359296 | bytes 9437216 | tf_op jit(solution)/shard_map/jit(_take)/select_n | solution.py:167
  131.3 15.6 %all-to-all-done.1 = bf16[16,2,192,1,64]{2,4,3,1,0:T(8,128)(2,1)S(1)} async-done(((bf16[16,2,192,1,64]{2,4,3,1,0:T(8,128)(2,1)}), bf16[16,2,192,1,64]{2,4,3,1,0:T(8,128)(2,1)S(1)}, u32[]{:S(2)}, u32[]{:S(2)}) %all-to-all-start.1) | async-done | bytes 786464 | tf_op jit(solution)/shard_map/all_to_all | solution.py:170
  146.9 5.0 %all-to-all-start.3 = ((bf16[16,2,192,1,384]{4,2,1,3,0:T(8,128)(2,1)}), bf16[16,2,192,1,384]{4,2,1,3,0:T(8,128)(2,1)}, u32[]{:S(2)}, u32[]{:S(2)}) async-start(bf16[16,2,192,1,384]{4,2,1,3,0:T(8,128)(2,1)} %select_bitcast_fusion), calls=%async_computation.3 | async-start | bytes 9437184 | tf_op jit(solution)/shard_map/all_to_all | solution.py:171
  152.2 0.1 copy.67
  152.4 0.9 copy.71
  153.3 1.4 copy.85
  154.7 0.5 convolution_bitcast_fusion
  155.2 0.2 reshape.173
  155.4 0.7 convert_add_fusion.1
  156.1 0.2 all-gather.5.cloned.1.call-start
  156.4 68.1 %all-gather.3.cloned.1.call-done = f32[1024,1024]{0,1:T(8,128)} async-done(((f32[1024,64]{0,1:T(8,128)}), f32[1024,1024]{0,1:T(8,128)}) %all-gather.3.cloned.1.call-update) | async-done | bytes 4194320 | tf_op jit(solution)/shard_map/all_gather | solution.py:198
  224.5 5.4 %copy.80.a_ref = f32[1024,1024]{1,0:T(8,128)} copy(f32[1024,1024]{0,1:T(8,128)} %all-gather.3.cloned.1.call-done) | data formatting | bytes 8388608 | tf_op jit(solution)/shard_map/all_gather | solution.py:198
  230.0 27.5 %all-to-all-done.3 = bf16[16,2,192,1,384]{4,2,1,3,0:T(8,128)(2,1)} async-done(((bf16[16,2,192,1,384]{4,2,1,3,0:T(8,128)(2,1)}), bf16[16,2,192,1,384]{4,2,1,3,0:T(8,128)(2,1)}, u32[]{:S(2)}, u32[]{:S(2)}) %all-to-all-start.3) | async-done | bytes 4718624 | tf_op jit(solution)/shard_map/all_to_all | solution.py:171
  257.4 7.0 %fusion.4 = f32[112,64,384]{2,0,1:T(8,128)S(1)} fusion(bf16[16,2,3,64,384]{4,3,2,1,0:T(8,128)(2,1)} %bitcast.23, s32[2,16,3]{1,2,0:T(4,128)S(1)} %copy.67), kind=kOutput, calls=%fused_computation.9 | convolution fusion | flops 528493056 | bytes 15729024 | tf_op jit(solution)/shard_map/ftuxw,tfup->pxw/dot_general | solution.py:195
  264.4 0.1 slice.35
  264.5 0.5 copy.79
  265.1 3.4 copy-done
  268.5 0.1 convert_add_fusion.p_ref
  268.6 67.3 %shard_map.85 = (f32[1024,64]{1,0:T(8,128)S(1)}, f32[1024,384]{1,0:T(8,128)}, bf16[1024,384]{1,0:T(8,128)(2,1)}) custom-call(f32[1024,1024]{1,0:T(8,128)} %copy.80.a_ref, f32[1024,384]{1,0:T(8,128)S(1)} %convert_add_fusion.p_ref), custom_call_target="tpu_custom_call" | custom-call | tf_op jit(solution)/shard_map/pallas_call | solution.py:87
  335.9 3.7 slice-done
  339.6 9.0 %copy.81 = f32[96,64,384]{2,1,0:T(8,128)} copy(f32[96,64,384]{2,0,1:T(8,128)S(1)} %slice-done) | data formatting | bytes 18874368 | tf_op jit(solution)/shard_map/slice | solution.py:202
  348.6 0.9 copy.82
  349.5 99.2 %all-gather.5.cloned.1.call-done = bf16[1024,6144]{1,0:T(8,128)(2,1)} async-done(((bf16[1024,384]{1,0:T(8,128)(2,1)}), bf16[1024,6144]{1,0:T(8,128)(2,1)}) %all-gather.5.cloned.1.call-update) | async-done | bytes 12582928 | tf_op jit(solution)/shard_map/all_gather | solution.py:208
  448.7 12.7 %fusion.1 = bf16[1,6144,384]{2,1,0:T(8,128)(2,1)} fusion(bf16[1024,6144]{1,0:T(8,128)(2,1)} %all-gather.5.cloned.1.call-done, bf16[1024,384]{1,0:T(8,128)(2,1)} %get-tuple-element.8, f32[96,64,384]{2,1,0:T(8,128)} %copy.81), kind=kOutput, calls=%fused_computation.4 | convolution fusion | flops 4836556800 | bytes 27525120 | tf_op jit(solution)/shard_map/dot_general | solution.py:207
  (25 shorter events, 0.6 us)
Async XLA Ops:
  18.7 25.1 %all-to-all-start = ((bf16[2,192,16,64]{1,3,0,2:T(8,128)(2,1)}), bf16[2,192,16,64]{1,3,0,2:T(8,128)(2,1)S(1)}, u32[]{:S(2)}, u32[]{:S(2)}) async-start(bf16[2,192,16,64]{1,3,0,2:T(8,128)(2,1)} %copy.70), calls=%async_computation | async-start | bytes 2097152 | tf_op jit(solution)/shard_map/all_to_all | solution.py:161
  43.8 68.1 %all-to-all-start.2 = ((bf16[2,192,16,384]{3,1,0,2:T(8,128)(2,1)}), bf16[2,192,16,384]{3,1,0,2:T(8,128)(2,1)}, u32[]{:S(2)}, u32[]{:S(2)}) async-start(bf16[2,192,16,384]{3,1,0,2:T(8,128)(2,1)} %copy.75), calls=%async_computation.2 | async-start | bytes 9437184 | tf_op jit(solution)/shard_map/all_to_all | solution.py:162
  111.9 35.1 %all-to-all-start.1 = ((bf16[16,2,192,1,64]{2,4,3,1,0:T(8,128)(2,1)}), bf16[16,2,192,1,64]{2,4,3,1,0:T(8,128)(2,1)S(1)}, u32[]{:S(2)}, u32[]{:S(2)}) async-start(bf16[16,2,192,1,64]{2,4,3,1,0:T(8,128)(2,1)} %broadcast_select_fusion), calls=%async_computation.1 | async-start | bytes 2097152 | tf_op jit(solution)/shard_map/all_to_all | solution.py:170
  146.9 110.5 %all-to-all-start.3 = ((bf16[16,2,192,1,384]{4,2,1,3,0:T(8,128)(2,1)}), bf16[16,2,192,1,384]{4,2,1,3,0:T(8,128)(2,1)}, u32[]{:S(2)}, u32[]{:S(2)}) async-start(bf16[16,2,192,1,384]{4,2,1,3,0:T(8,128)(2,1)} %select_bitcast_fusion), calls=%async_computation.3 | async-start | bytes 9437184 | tf_op jit(solution)/shard_map/all_to_all | solution.py:171
  151.9 3.4 copy-start.2
  151.9 72.6 %all-gather.3.cloned.1.call-start = ((), (), s32[]{:S(2)}) async-start(), calls=%async_computation.4 | async-start | bytes 4456448 | tf_op jit(solution)/shard_map/all_gather | solution.py:198
  156.1 292.5 %all-gather.5.cloned.1.call-start = ((), (), s32[]{:S(2)}) async-start(), calls=%async_computation.5 | async-start | bytes 13369344 | tf_op jit(solution)/shard_map/all_gather | solution.py:208
  264.4 4.0 copy-start
  264.4 4.0 copy-start.1
  335.9 3.7 slice-start
Sparse Core Ops, SparseCore 0:
  156.3 68.2 all-gather.2
  336.0 112.5 all-gather.4

commit v2 on v0

v2 whole, which is shorter than its diff:
```python
import functools

import jax
import jax.numpy as jnp
from jax import lax
from jax.experimental import pallas as pl
from jax.experimental.pallas import tpu as pltpu
from jax.sharding import PartitionSpec as P

N = 1024
NB = 128
PC = 384
WT = N + PC
SLOTS = 56
KB = 24
KIDS = 32
F32 = jnp.float32
BF = jnp.bfloat16
MESH = pl.DeviceIdType.MESH


def vm():
    return pl.BlockSpec(memory_space=pltpu.VMEM)


def sm():
    return pl.BlockSpec(memory_space=pltpu.SMEM)


def split(x):
    hi = x.astype(BF)
    return hi, (x - hi.astype(F32)).astype(BF)


def dg(a, b, ca, cb):
    return lax.dot_general(a, b, (((ca,), (cb,)), ((), ())), preferred_element_type=F32)


def kid_order_table(parent_ref, order, count):
    for p in range(KIDS // 2):
        count[p] = 0
    for c in range(KIDS):
        p = parent_ref[c]
        n = count[p]
        order[2 * p + n] = c
        count[p] = n + 1


def slot_table(child, parent, map_ref, piv_ref, tab, slots, base):
    for v in range(SLOTS):
        tab[v] = -1
    for a in range(KB):
        tab[map_ref[child, a]] = a
    for s in range(SLOTS):
        slots[base + s] = tab[piv_ref[parent, s]]


def pack_kernel(x_ref, map_ref, parent_ref, piv_ref, pan_ref, t0_ref, t1_ref, t2_ref, tab, slots):
    g = lax.axis_index("grid")
    for k in range(2):
        c = 2 * g + k
        slot_table(c, parent_ref[c], map_ref, piv_ref, tab, slots, k * SLOTS)
    lane = lax.broadcasted_iota(jnp.int32, (192, NB), 1)

    def block(k, slot):
        a = slots[k * SLOTS + slot]
        off = pl.multiple_of(jnp.maximum(a, 0) * NB, NB)
        x = x_ref[k, :, pl.ds(off, NB)]
        return jnp.where(a >= 0, x, jnp.zeros_like(x))

    def panel(j, carry):
        x0 = block(0, j).astype(F32)
        x1 = block(1, j).astype(F32)
        r0 = pltpu.roll(x0, 64, 1)
        r1 = pltpu.roll(x1, 64, 1)
        pan_ref[2 * j] = jnp.where(lane < 64, x0, r1).astype(BF)
        pan_ref[2 * j + 1] = jnp.where(lane < 64, r0, x1).astype(BF)
        return carry

    lax.fori_loop(0, 8, panel, 0)

    def trail(m, carry):
        for k in range(2):
            for i in range(3):
                x = block(k, 8 + 3 * m + i)
                for s, t_ref in enumerate((t0_ref, t1_ref, t2_ref)):
                    t_ref[m, k, :, i * NB : (i + 1) * NB] = x[64 * s : 64 * s + 64]
        return carry

    lax.fori_loop(0, 16, trail, 0)


def pack(x, child_map, child_parent, pivot_order):
    t = jax.ShapeDtypeStruct((16, 2, 64, PC), BF)
    return pl.pallas_call(
        pack_kernel,
        out_shape=(jax.ShapeDtypeStruct((16, 192, NB), BF), t, t, t),
        in_specs=[vm(), sm(), sm(), sm()],
        out_specs=(vm(), vm(), vm(), vm()),
        scratch_shapes=[pltpu.SMEM((SLOTS,), jnp.int32), pltpu.SMEM((2 * SLOTS,), jnp.int32)],
        compiler_params=pltpu.CompilerParams(vmem_limit_bytes=40 << 20),
        name="pack",
    )(x, child_map, child_parent, pivot_order)


def sort_panel_kernel(x_ref, parent_ref, o_ref, order, count):
    kid_order_table(parent_ref, order, count)
    lane = lax.broadcasted_iota(jnp.int32, (192, NB), 1)

    def one(p, carry):
        c0 = order[2 * p]
        c1 = order[2 * p + 1]
        x0 = x_ref[c0 // 2].astype(F32)
        x1 = x_ref[c1 // 2].astype(F32)
        x0 = jnp.where(c0 % 2 == 0, x0, pltpu.roll(x0, 64, 1))
        x1 = jnp.where(c1 % 2 == 1, x1, pltpu.roll(x1, 64, 1))
        o_ref[p] = jnp.where(lane < 64, x0, x1).astype(BF)
        return carry

    lax.fori_loop(0, 16, one, 0)


def sort_trail_kernel(x_ref, parent_ref, o_ref, order, count):
    kid_order_table(parent_ref, order, count)

    def one(p, carry):
        for t in range(2):
            c = order[2 * p + t]
            o_ref[p, t] = x_ref[c // 2, c % 2]
        return carry

    lax.fori_loop(0, 16, one, 0)


def sort_call(kernel, x, child_parent, name):
    return pl.pallas_call(
        kernel,
        out_shape=jax.ShapeDtypeStruct(x.shape, x.dtype),
        in_specs=[vm(), sm()],
        out_specs=vm(),
        scratch_shapes=[pltpu.SMEM((KIDS,), jnp.int32), pltpu.SMEM((KIDS // 2,), jnp.int32)],
        compiler_params=pltpu.CompilerParams(vmem_limit_bytes=20 << 20),
        name=name,
    )(x, child_parent)


def own_slots(parent_ref, map_ref, piv_ref, tab, slots, order, count):
    f = lax.axis_index("front")
    kid_order_table(parent_ref, order, count)
    for t in range(2):
        slot_table(order[2 * f + t], f, map_ref, piv_ref, tab, slots, t * SLOTS)


def rows_kernel(x_ref, od_ref, map_ref, parent_ref, piv_ref, d_ref, p_ref, tab, slots, order, count):
    own_slots(parent_ref, map_ref, piv_ref, tab, slots, order, count)

    def block(slot):
        halves = []
        for v in range(2):
            total = jnp.zeros((64, NB), F32)
            for t in range(2):
                a = slots[t * SLOTS + slot]
                u = 2 * jnp.maximum(a, 0) + v
                x = x_ref[u // 3, pl.ds(pl.multiple_of((u % 3) * 64, 64), 64), :].astype(F32)
                if t == 1:
                    x = pltpu.roll(x, 64, 1)
                total = total + jnp.where(a >= 0, x, 0.0)
            halves.append(total)
        return jnp.transpose(jnp.concatenate(halves, 0))[:64]

    for j in range(8):
        od = od_ref[0, j * NB : (j + 1) * NB, :].astype(F32)
        od = jnp.transpose(od)
        d_ref[:, j * NB : (j + 1) * NB] = block(j) + od

    def trail(m, carry):
        for i in range(3):
            p_ref[m, :, i * NB : (i + 1) * NB] = block(8 + 3 * m + i)
        return carry

    lax.fori_loop(0, 16, trail, 0)


def pivot_rows(x, orig_diag, child_map, child_parent, pivot_order):
    return pl.pallas_call(
        rows_kernel,
        out_shape=(
            jax.ShapeDtypeStruct((64, N), F32),
            jax.ShapeDtypeStruct((16, 64, PC), F32),
        ),
        in_specs=[vm(), vm(), sm(), sm(), sm()],
        out_specs=(vm(), vm()),
        scratch_shapes=[
            pltpu.SMEM((SLOTS,), jnp.int32),
            pltpu.SMEM((2 * SLOTS,), jnp.int32),
            pltpu.SMEM((KIDS,), jnp.int32),
            pltpu.SMEM((KIDS // 2,), jnp.int32),
        ],
        compiler_params=pltpu.CompilerParams(vmem_limit_bytes=20 << 20),
        name="pivot_rows",
    )(x, orig_diag, child_map, child_parent, pivot_order)


def factor_block(m_ref, inv_ref):
    rid = lax.broadcasted_iota(jnp.int32, (8, 1), 0)
    rows = [m_ref[8 * r : 8 * r + 8, :] for r in range(16)]
    for q in range(16):
        c0 = 8 * q
        rb = [jnp.broadcast_to(rows[q][s : s + 1, :], (8, 2 * NB)) for s in range(8)]
        e = [
            [
                jnp.broadcast_to(rb[s][:, c0 + t : c0 + t + 1], (8, NB)) if t >= s else None
                for t in range(8)
            ]
            for s in range(8)
        ]
        inv = [None] * 8
        for t in range(8):
            inv[t] = 1.0 / e[t][t]
            for s in range(t + 1, 8):
                m = e[t][s] * inv[t]
                for u in range(s, 8):
                    e[s][u] = e[s][u] - m * e[t][u]
                rb[s] = rb[s] - jnp.concatenate([m, m], 1) * rb[t]
        new, iv = rb[7], inv[7]
        for s in range(6, -1, -1):
            new = jnp.where(rid == s, rb[s], new)
            iv = jnp.where(rid == s, inv[s], iv)
        m_ref[c0 : c0 + 8, :] = new
        inv_ref[c0 : c0 + 8, :] = iv
        if q < 15:
            cols = jnp.transpose(new[:, :NB] * iv)
            for r in range(q + 1, 16):
                p = [cols[8 * r : 8 * r + 8, t : t + 1] * rb[t] for t in range(8)]
                rows[r] = rows[r] - (
                    ((p[0] + p[1]) + (p[2] + p[3])) + ((p[4] + p[5]) + (p[6] + p[7]))
                )


class Gather:
    def __init__(self, own, out, send, recv, rows):
        self.own, self.out, self.send, self.recv, self.half = own, out, send, recv, rows // 2
        self.f = lax.axis_index("front")
        g = lax.axis_index("grid")
        self.x, self.y = g // 4, g % 4

    def dev(self, axis, d):
        if axis == 0:
            return (self.f, lax.rem(self.x + d, 4) * 4 + self.y)
        return (self.f, self.x * 4 + lax.rem(self.y + d, 4))

    def at(self, axis, d, r0, rn):
        x, y = self.x, self.y
        if axis == 0:
            x = lax.rem(x + d, 4)
        else:
            y = lax.rem(y + d, 4)
        return self.out.at[x, y, pl.ds(r0, rn), :]

    def line(self, axis, d, r0, rn):
        if axis == 0:
            return self.out.at[lax.rem(self.x + d, 4), :, pl.ds(r0, rn), :]
        return self.out.at[:, lax.rem(self.y + d, 4), pl.ds(r0, rn), :]

    def copy(self, src, dst, sem, axis, d):
        return pltpu.make_async_remote_copy(
            src_ref=src,
            dst_ref=dst,
            send_sem=self.send.at[sem],
            recv_sem=self.recv.at[sem],
            device_id=self.dev(axis, d),
            device_id_type=MESH,
        )

    def stage(self, n):
        h = self.half
        q = h // 2
        out = []
        for axis in range(2):
            r0 = axis * h
            other = 1 - axis
            b = axis * 8 + 2 * n
            if n == 0:
                src = self.own.at[pl.ds(r0, h), :]
                out.append(self.copy(src, self.at(axis, 0, r0, h), b, axis, 1))
                out.append(self.copy(src, self.at(axis, 0, r0, h), b + 1, axis, 3))
            elif n == 1:
                a = self.at(axis, 3, r0, q)
                out.append(self.copy(a, a, b, axis, 1))
                a = self.at(axis, 1, r0 + q, q)
                out.append(self.copy(a, a, b + 1, axis, 3))
            elif n == 2:
                a = self.line(other, 0, r0, h)
                out.append(self.copy(a, a, b, other, 1))
                out.append(self.copy(a, a, b + 1, other, 3))
            else:
                a = self.line(other, 3, r0, q)
                out.append(self.copy(a, a, b, other, 1))
                a = self.line(other, 1, r0 + q, q)
                out.append(self.copy(a, a, b + 1, other, 3))
        return out

    def start(self, n):
        for c in self.stage(n):
            c.start()

    def wait_recv(self, n):
        for c in self.stage(n):
            c.wait_recv()

    def wait_send(self):
        for n in range(4):
            for c in self.stage(n):
                c.wait_send()


def lu_kernel(
    d_ref, p_ref, or_ref, ud_ref, ur_ref, s_ref, sg_ref,
    w, m_ref, inv_ref, uh, ul, st, dall, dsend, drecv, ssend, srecv, lsem,
):
    f = lax.axis_index("front")
    g = lax.axis_index("grid")
    x, y = g // 4, g % 4
    barrier = pltpu.get_barrier_semaphore()
    for dx, dy in ((1, 0), (3, 0), (0, 1), (0, 3)):
        other = lax.rem(x + dx, 4) * 4 + lax.rem(y + dy, 4)
        pl.semaphore_signal(barrier, inc=1, device_id=(f, other), device_id_type=MESH)
    pl.semaphore_wait(barrier, 4)
    gd = Gather(d_ref, dall, dsend, drecv, 64)
    gd.start(0)
    dall[x, y] = d_ref[...]
    w[:, N:] = p_ref[...] + or_ref[0].astype(F32)
    for n in range(3):
        gd.wait_recv(n)
        gd.start(n + 1)
    gd.wait_recv(3)
    gd.wait_send()
    for i in range(16):
        w[64 * i : 64 * i + 64, :N] = dall[i // 4, i % 4]
    eye = (
        lax.broadcasted_iota(jnp.int32, (NB, NB), 0) == lax.broadcasted_iota(jnp.int32, (NB, NB), 1)
    ).astype(F32)

    def gs(k):
        return Gather(st.at[k], sg_ref.at[k], ssend.at[k], srecv.at[k], PC)

    def local(k):
        return pltpu.make_async_copy(st.at[k], sg_ref.at[k, x, y], lsem.at[k])

    def move(k, n):
        c = gs(k)
        c.wait_recv(n - 1)
        if n == 2:
            local(k).wait()
        c.start(n)

    def step(k, carry):
        r0 = pl.multiple_of(k * NB, NB)
        m_ref[:, :NB] = w[pl.ds(r0, NB), pl.ds(r0, NB)]
        m_ref[:, NB:] = eye
        factor_block(m_ref, inv_ref)

        @pl.when(k >= 1)
        def _():
            move(k - 1, 1)

        @pl.when(k >= 2)
        def _():
            move(k - 2, 3)

        lh, ll = split(m_ref[:, NB:])
        ah, al = split(w[pl.ds(r0, NB), :])
        u = dg(lh, ah, 1, 0) + (dg(lh, al, 1, 0) + dg(ll, ah, 1, 0))
        w[pl.ds(r0, NB), :] = u
        h, l = split(u)
        uh[...] = h
        ul[...] = l
        iv = inv_ref[...]
        top = u[:, N:]
        ur_ref[pl.ds(r0, NB), :] = top
        rs = jnp.sqrt(iv)
        solved = top * jnp.concatenate([rs] * 3, 1)
        s_ref[pl.ds(r0, NB), :] = solved.astype(BF)
        st[k] = jnp.transpose(solved).astype(BF)
        gs(k).start(0)
        local(k).start()

        def upd(i, c):
            i0 = pl.multiple_of(i * NB, NB)
            xh, xl = split((uh[:, pl.ds(i0, NB)].astype(F32) + ul[:, pl.ds(i0, NB)].astype(F32)) * iv)
            d = dg(xh, uh[...], 0, 0) + (dg(xh, ul[...], 0, 0) + dg(xl, uh[...], 0, 0))
            w[pl.ds(i0, NB), :] = w[pl.ds(i0, NB), :] - d
            return c

        lax.fori_loop(k + 1, N // NB, upd, 0)

        @pl.when(k >= 1)
        def _():
            move(k - 1, 2)

        return carry

    last = N // NB - 1
    lax.fori_loop(0, N // NB, step, 0)
    move(last, 1)
    move(last - 1, 3)
    move(last, 2)
    blk = pl.multiple_of((g // 2) * NB, NB)
    own = w[:, pl.ds(blk, NB)]
    own = jnp.where(g % 2 == 1, own[:, 64:], own[:, :64])
    col = 64 * g + lax.broadcasted_iota(jnp.int32, (N, 64), 1)
    ud_ref[...] = jnp.where(lax.broadcasted_iota(jnp.int32, (N, 64), 0) <= col, own, 0.0)
    move(last, 3)

    def finish(k, carry):
        c = gs(k)
        c.wait_recv(3)
        c.wait_send()
        return carry

    lax.fori_loop(0, N // NB, finish, 0)


def lu_call(d, p, orig_rows):
    steps = N // NB
    return pl.pallas_call(
        lu_kernel,
        out_shape=(
            jax.ShapeDtypeStruct((N, 64), F32),
            jax.ShapeDtypeStruct((N, PC), F32),
            jax.ShapeDtypeStruct((N, PC), BF),
            jax.ShapeDtypeStruct((steps, 4, 4, PC, NB), BF),
        ),
        in_specs=[vm(), vm(), vm()],
        out_specs=(vm(), vm(), vm(), pl.BlockSpec(memory_space=pl.ANY)),
        scratch_shapes=[
            pltpu.VMEM((N, WT), F32),
            pltpu.VMEM((NB, 2 * NB), F32),
            pltpu.VMEM((NB, NB), F32),
            pltpu.VMEM((NB, WT), BF),
            pltpu.VMEM((NB, WT), BF),
            pltpu.VMEM((steps, PC, NB), BF),
            pltpu.VMEM((4, 4, 64, N), F32),
            pltpu.SemaphoreType.DMA((16,)),
            pltpu.SemaphoreType.DMA((16,)),
            pltpu.SemaphoreType.DMA((steps, 16)),
            pltpu.SemaphoreType.DMA((steps, 16)),
            pltpu.SemaphoreType.DMA((steps,)),
        ],
        compiler_params=pltpu.CompilerParams(
            vmem_limit_bytes=48 << 20, collective_id=0, has_side_effects=True
        ),
        cost_estimate=pl.CostEstimate(flops=3 * 10**9, bytes_accessed=300 * 10**6, transcendentals=0),
        name="factor_gather",
    )(d, p, orig_rows)


def schur_kernel(
    sg_ref, s_ref, t0_ref, t1_ref, t2_ref, map_ref, parent_ref, piv_ref, o_ref, tab, slots, order, count
):
    m = pl.program_id(0)

    @pl.when(m == 0)
    def _():
        own_slots(parent_ref, map_ref, piv_ref, tab, slots, order, count)

    lhs = jnp.concatenate([sg_ref[k, 0] for k in range(N // NB)], 1)
    prod = dg(lhs, s_ref[...], 1, 0)
    for i in range(3):
        for v in range(2):
            total = -prod[i * NB + v * 64 : i * NB + v * 64 + 64]
            for t in range(2):
                a = slots[t * SLOTS + 8 + 3 * m + i]
                u = 2 * jnp.maximum(a, 0) + v
                s = u % 3
                x = jnp.where(
                    s == 0, t0_ref[u // 3, t], jnp.where(s == 1, t1_ref[u // 3, t], t2_ref[u // 3, t])
                )
                total = total + jnp.where(a >= 0, x.astype(F32), 0.0)
            o_ref[0, i * NB + v * 64 : i * NB + v * 64 + 64, :] = total.astype(BF)


def schur_call(sg, s, t0, t1, t2, child_map, child_parent, pivot_order):
    steps = N // NB
    return pl.pallas_call(
        schur_kernel,
        out_shape=jax.ShapeDtypeStruct((1, 16 * PC, PC), BF),
        grid=(16,),
        in_specs=[
            pl.BlockSpec((steps, 1, PC, NB), lambda m: (0, m, 0, 0)),
            vm(), vm(), vm(), vm(), sm(), sm(), sm(),
        ],
        out_specs=pl.BlockSpec((1, PC, PC), lambda m: (0, m, 0)),
        scratch_shapes=[
            pltpu.SMEM((SLOTS,), jnp.int32),
            pltpu.SMEM((2 * SLOTS,), jnp.int32),
            pltpu.SMEM((KIDS,), jnp.int32),
            pltpu.SMEM((KIDS // 2,), jnp.int32),
        ],
        compiler_params=pltpu.CompilerParams(vmem_limit_bytes=40 << 20),
        name="schur",
    )(sg.reshape(steps, 16, PC, NB), s, t0, t1, t2, child_map, child_parent, pivot_order)


def exchange(x, axis):
    return lax.all_to_all(x, axis, split_axis=0, concat_axis=0, tiled=True)


def shards(child_blocks, orig_diag, orig_rows, child_map, child_parent, pivot_order):
    tables = (child_map, child_parent, pivot_order)
    panel, *trail = pack(child_blocks, *tables)
    panel = exchange(panel, "grid")
    trail = [exchange(t, "grid") for t in trail]
    panel = exchange(sort_call(sort_panel_kernel, panel, child_parent, "sort_panel"), "front")
    trail = [
        exchange(sort_call(sort_trail_kernel, t, child_parent, "sort_trail"), "front") for t in trail
    ]
    d, p = pivot_rows(panel, orig_diag, *tables)
    p = exchange(p, "grid").reshape(N, PC)
    upper_diag, upper_rows, s, sg = lu_call(d, p, orig_rows)
    schur = schur_call(sg, s, *trail, *tables)
    return upper_diag[None], upper_rows[None], schur


def solution(mesh):
    return jax.shard_map(
        shards,
        mesh=mesh,
        in_specs=(
            P("grid", "front", None),
            P("front", None, "grid"),
            P("front", None, "grid"),
            P(),
            P(),
            P(),
        ),
        out_specs=(P("front", None, "grid"), P("front", None, "grid"), P("front", None, "grid")),
        check_vma=False,
    )
```

time: 698 us -> 417 us (0.60); the launches traced: 689 us -> 415 us
  other arithmetic: 277 us -> 0 us
  Pallas kernels: 0 us -> 167 us
  local copies, waits for them, and re-layouts: 101 us -> 19.7 us
  waiting for transfers between devices: 197 us -> 121 us
  blocking collectives: 0 us -> 75.3 us
  matrix products: 64.2 us -> 0 us
  between operations: 20.4 us -> 0.82 us
    another operation x34 -> x0, other arithmetic: 258 us -> none  [the longest x31 173 us: shards(): lower_factor = jnp.linalg.cholesky(pivot_whole)]
    pallas_call x0 -> x8, Pallas kernels: none -> 167 us  [the longest x1 133 us: lu_call(): pl.pallas_call(lu_kernel, out_shape=(jax.ShapeDtypeStruct((N, 64), F32),...]
    all_gather x2 -> x0, waiting for transfers between devices: 81 us -> none  [the longest x1 80.9 us: shards(): lax.all_gather(rounded, 'grid', axis=1, tiled=True)]
    all_to_all x0 -> x3, blocking collectives: none -> 75.3 us  [exchange(): return lax.all_to_all(x, axis, split_axis=0, concat_axis=0, tiled=True)]
    another operation x29 -> x0, matrix products: 37.5 us -> none  [the longest x14 23.1 us: shards(): lower_factor = jnp.linalg.cholesky(pivot_whole)]
    dot_general x5 -> x0, matrix products: 26.7 us -> none  [the longest x1 12.6 us: shards(): lax.dot_general(lax.all_gather(rounded, 'grid', axis=1, tiled=True), roun...]
    another operation x36 -> x0, local copies, waits for them, and re-layouts: 25.7 us -> none
    gather x3 -> x0, local copies, waits for them, and re-layouts: 25 us -> none  [the longest x1 17.4 us: shards(): pivots = jnp.diagonal(lower_factor)]
  transfers between devices with their start and end apart: 6 -> 6, of which waited for: 4 -> 5; matrix products, arithmetic and copies ran while one was open for 55% -> 1% of each run, Pallas kernels for 0% -> 35%
where the time goes in v2:
time: 417 us; the launch traced here: 415 us
  Pallas kernels  167 us (40%)
  waiting for transfers between devices  121 us (29%)
  blocking collectives  75.3 us (18%)
  starting transfers between devices  32 us (8%)
  local copies, waits for them, and re-layouts  19.7 us (5%)
    pallas_call x1, Pallas kernels, lu_call(): pl.pallas_call(lu_kernel, out_shape=(jax.ShapeDtypeStruct((N, 64), F32),...  133 us
    all_to_all x6, waiting for transfers between devices, exchange(): return lax.all_to_all(x, axis, split_axis=0, concat_axis=0, tiled=True)  121 us
    all_to_all x3, blocking collectives, exchange(): return lax.all_to_all(x, axis, split_axis=0, concat_axis=0, tiled=True)  75.3 us
    all_to_all x6, starting transfers between devices, exchange(): return lax.all_to_all(x, axis, split_axis=0, concat_axis=0, tiled=True)  32 us
    unnamed x44, local copies, waits for them, and re-layouts  19.7 us
    pallas_call x1, Pallas kernels, schur_call(): pl.pallas_call(schur_kernel, out_shape=jax.ShapeDtypeStruct((1, 16 * PC,...  18 us
  transfers between devices with their start and end apart: 6, of which 5 were waited for; matrix products, arithmetic and copies ran while one was open for 1% of the time, Pallas kernels for 35%

profile of v2, /device:TPU:2, one launch (start us, length us, event | category | flops | bytes accessed | tf_op | source)
XLA Modules:
  0.0 415.2 jit_solution(2671846769038725214)
XLA Ops:
  0.6 0.8 copy.9.map_ref
  1.4 1.7 copy-done.4
  3.1 0.7 copy-done.13
  3.8 0.7 copy-done.15
  4.4 3.4 pack.1
  7.9 0.0 copy-start.5
  7.9 0.0 copy-start.9
  7.9 19.7 %all_to_all.45.x_ref = bf16[16,192,128]{2,1,0:T(8,128)(2,1)S(1)} all-to-all(bf16[16,192,128]{2,1,0:T(8,128)(2,1)S(1)} %get-tuple-element.13), channel_id=1, replica_groups=mesh['front'=16,'grid'=16] {'grid'}, dimensions={0} | all-to-all | bytes 1572864 | tf_op jit(solution)/shard_map/all_to_all | solution.py:506
  27.6 24.7 %all_to_all.46.x_ref = bf16[16,2,64,384]{3,2,1,0:T(8,128)(2,1)} all-to-all(bf16[16,2,64,384]{3,2,1,0:T(8,128)(2,1)S(1)} %get-tuple-element.20), channel_id=1, replica_groups=mesh['front'=16,'grid'=16] {'grid'}, dimensions={0} | all-to-all | bytes 3145728 | tf_op jit(solution)/shard_map/all_to_all | solution.py:506
  52.4 6.0 %all-to-all-start.5 = ((bf16[16,2,64,384]{3,2,1,0:T(8,128)(2,1)}), bf16[16,2,64,384]{3,2,1,0:T(8,128)(2,1)S(1)}, u32[]{:S(2)}, u32[]{:S(2)}) async-start(bf16[16,2,64,384]{3,2,1,0:T(8,128)(2,1)} %copy-done.9), calls=%async_computation.5 | async-start | bytes 3145728 | tf_op jit(solution)/shard_map/all_to_all | solution.py:506
  58.4 2.4 sort_panel.1
  60.8 17.0 %all-to-all-done.5.x_ref = bf16[16,2,64,384]{3,2,1,0:T(8,128)(2,1)S(1)} async-done(((bf16[16,2,64,384]{3,2,1,0:T(8,128)(2,1)}), bf16[16,2,64,384]{3,2,1,0:T(8,128)(2,1)S(1)}, u32[]{:S(2)}, u32[]{:S(2)}) %all-to-all-start.5) | async-done | bytes 1572896 | tf_op jit(solution)/shard_map/all_to_all | solution.py:506
  77.8 30.8 %all_to_all.47.x_ref = bf16[16,192,128]{2,1,0:T(8,128)(2,1)} all-to-all(bf16[16,192,128]{2,1,0:T(8,128)(2,1)S(1)} %sort_panel.1), channel_id=1, replica_groups=mesh['front'=16,'grid'=16] {'front'}, dimensions={0} | all-to-all | bytes 1572864 | tf_op jit(solution)/shard_map/all_to_all | solution.py:506
  108.6 5.6 %all-to-all-start.7 = ((bf16[16,2,64,384]{3,2,1,0:T(8,128)(2,1)}), bf16[16,2,64,384]{3,2,1,0:T(8,128)(2,1)S(1)}, u32[]{:S(2)}, u32[]{:S(2)}) async-start(bf16[16,2,64,384]{3,2,1,0:T(8,128)(2,1)} %copy-done.5), calls=%async_computation.7 | async-start | bytes 3145728 | tf_op jit(solution)/shard_map/all_to_all | solution.py:506
  114.2 1.1 copy.10.od_ref
  115.3 1.1 copy-done.3
  116.4 5.0 %pivot_rows.1 = (f32[64,1024]{1,0:T(8,128)S(1)}, f32[16,64,384]{2,1,0:T(8,128)S(1)}) custom-call(bf16[16,192,128]{2,1,0:T(8,128)(2,1)S(1)} %copy-done.3, bf16[1,1024,64]{2,1,0:T(8,128)(2,1)S(1)} %copy.10.od_ref, s32[32,24]{1,0:T(8,128)S(1)} %copy.9.map_ref, s32[32]{0:T(128)S(1)} %copy-done.16, s32[16,56]{1,0:T(8,128)S(1)} %copy-done.14), custom_call_target="tpu_custom_call" | custom-call | tf_op jit(solution)/shard_map/pivot_rows/pallas_call | solution.py:185
  121.4 0.0 copy-start.8
  121.4 1.1 copy-done.8
  122.6 0.7 copy-done.18
  123.3 14.6 %all-to-all-done.7.x_ref = bf16[16,2,64,384]{3,2,1,0:T(8,128)(2,1)S(1)} async-done(((bf16[16,2,64,384]{3,2,1,0:T(8,128)(2,1)}), bf16[16,2,64,384]{3,2,1,0:T(8,128)(2,1)S(1)}, u32[]{:S(2)}, u32[]{:S(2)}) %all-to-all-start.7) | async-done | bytes 1572896 | tf_op jit(solution)/shard_map/all_to_all | solution.py:506
  137.9 6.5 %all-to-all-start.2 = ((f32[16,64,384]{2,1,0:T(8,128)}), f32[16,64,384]{2,1,0:T(8,128)}, u32[]{:S(2)}, u32[]{:S(2)}) async-start(f32[16,64,384]{2,1,0:T(8,128)} %copy-done.8), calls=%async_computation.2 | async-start | bytes 3145728 | tf_op jit(solution)/shard_map/all_to_all | solution.py:506
  144.4 1.4 copy-done
  145.8 1.2 sort_trail.3
  146.9 0.0 copy-start.1
  146.9 1.1 copy-done.1
  148.1 17.8 %all-to-all-done.2 = f32[16,64,384]{2,1,0:T(8,128)} async-done(((f32[16,64,384]{2,1,0:T(8,128)}), f32[16,64,384]{2,1,0:T(8,128)}, u32[]{:S(2)}, u32[]{:S(2)}) %all-to-all-start.2) | async-done | bytes 1572896 | tf_op jit(solution)/shard_map/all_to_all | solution.py:506
  165.9 4.4 %all-to-all-start.4 = ((bf16[16,2,64,384]{3,2,1,0:T(8,128)(2,1)}), bf16[16,2,64,384]{3,2,1,0:T(8,128)(2,1)}, u32[]{:S(2)}, u32[]{:S(2)}) async-start(bf16[16,2,64,384]{3,2,1,0:T(8,128)(2,1)} %copy-done.1), calls=%async_computation.4 | async-start | bytes 3145728 | tf_op jit(solution)/shard_map/all_to_all | solution.py:506
  170.3 1.2 sort_trail.4
  171.5 0.0 copy-start.2
  171.5 1.1 copy-done.2
  172.6 35.6 %all-to-all-done.4.t0_ref = bf16[16,2,64,384]{3,2,1,0:T(8,128)(2,1)} async-done(((bf16[16,2,64,384]{3,2,1,0:T(8,128)(2,1)}), bf16[16,2,64,384]{3,2,1,0:T(8,128)(2,1)}, u32[]{:S(2)}, u32[]{:S(2)}) %all-to-all-start.4) | async-done | bytes 1572896 | tf_op jit(solution)/shard_map/all_to_all | solution.py:506
  208.2 4.8 %all-to-all-start.6 = ((bf16[16,2,64,384]{3,2,1,0:T(8,128)(2,1)}), bf16[16,2,64,384]{3,2,1,0:T(8,128)(2,1)S(1)}, u32[]{:S(2)}, u32[]{:S(2)}) async-start(bf16[16,2,64,384]{3,2,1,0:T(8,128)(2,1)} %copy-done.2), calls=%async_computation.6 | async-start | bytes 3145728 | tf_op jit(solution)/shard_map/all_to_all | solution.py:506
  213.0 2.3 sort_trail.5
  215.3 35.6 %all-to-all-done.6.t1_ref = bf16[16,2,64,384]{3,2,1,0:T(8,128)(2,1)S(1)} async-done(((bf16[16,2,64,384]{3,2,1,0:T(8,128)(2,1)}), bf16[16,2,64,384]{3,2,1,0:T(8,128)(2,1)S(1)}, u32[]{:S(2)}, u32[]{:S(2)}) %all-to-all-start.6) | async-done | bytes 1572896 | tf_op jit(solution)/shard_map/all_to_all | solution.py:506
  250.8 4.8 %all-to-all-start.8 = ((bf16[16,2,64,384]{3,2,1,0:T(8,128)(2,1)}), bf16[16,2,64,384]{3,2,1,0:T(8,128)(2,1)S(1)}, u32[]{:S(2)}, u32[]{:S(2)}) async-start(bf16[16,2,64,384]{3,2,1,0:T(8,128)(2,1)} %sort_trail.5), calls=%async_computation.8 | async-start | bytes 3145728 | tf_op jit(solution)/shard_map/all_to_all | solution.py:506
  255.6 0.0 copy-start.17
  255.6 1.1 copy-done.17
  256.8 133.3 %factor_gather.1 = (f32[1024,64]{1,0:T(8,128)S(1)}, f32[1024,384]{1,0:T(8,128)S(1)}, bf16[1024,384]{1,0:T(8,128)(2,1)S(1)}, bf16[8,4,4,384,128]{4,3,2,1,0:T(8,128)(2,1)}) custom-call(f32[64,1024]{1,0:T(8,128)S(1)} %copy-done.19, f32[1024,384]{1,0:T(8,128)} %bitcast.p_ref, bf16[1,1024,384]{2,1,0:T(8,128)(2,1)S(1)} %copy-done.17), custom_call_target="tpu_custom_call" | custom-call | flops 3000000000 | bytes 300000000 | tf_op jit(solution)/shard_map/factor_gather/pallas_call | solution.py:426
  390.1 0.0 copy-start.6
  390.1 1.1 copy-done.6
  391.2 0.9 copy-done.10
  392.1 0.8 copy-done.12
  393.0 1.9 copy.13
  394.9 0.0 all-to-all-done.8.t2_ref
  394.9 1.1 copy-done.11
  396.0 18.0 %schur.1 = bf16[1,6144,384]{2,1,0:T(8,128)(2,1)} custom-call(bf16[8,16,384,128]{3,2,1,0:T(8,128)(2,1)} %bitcast.6, bf16[1024,384]{1,0:T(8,128)(2,1)S(1)} %copy-done.11, bf16[16,2,64,384]{3,2,1,0:T(8,128)(2,1)} %all-to-all-done.4.t0_ref, bf16[16,2,64,384]{3,2,1,0:T(8,128)(2,1)S(1)} %all-to-all-done.6.t1_ref, ...), custom_call_target="tpu_custom_call" | custom-call | tf_op jit(solution)/shard_map/schur/pallas_call | solution.py:485
  414.0 1.1 copy.15
  (19 shorter events, 0.0 us)
Async XLA Ops:
  1.4 1.7 copy-start.4
  3.1 0.7 copy-start.13
  3.8 0.7 copy-start.15
  7.9 44.5 %copy-start.5 = (bf16[16,2,64,384]{3,2,1,0:T(8,128)(2,1)}, bf16[16,2,64,384]{3,2,1,0:T(8,128)(2,1)S(1)}, u32[]{:S(2)}) copy-start(bf16[16,2,64,384]{3,2,1,0:T(8,128)(2,1)S(1)} %get-tuple-element.22) | copy-start | bytes 4718596
  7.9 44.5 %copy-start.9 = (bf16[16,2,64,384]{3,2,1,0:T(8,128)(2,1)}, bf16[16,2,64,384]{3,2,1,0:T(8,128)(2,1)S(1)}, u32[]{:S(2)}) copy-start(bf16[16,2,64,384]{3,2,1,0:T(8,128)(2,1)S(1)} %get-tuple-element.21) | copy-start | bytes 4718596
  52.3 6.0 %copy-start.16 = (s32[32]{0:T(128)S(1)}, s32[32]{0:T(128)}, u32[]{:S(2)}) copy-start(s32[32]{0:T(128)} %parent_ref.13) | copy-start | bytes 388
  52.4 25.5 %all-to-all-start.5 = ((bf16[16,2,64,384]{3,2,1,0:T(8,128)(2,1)}), bf16[16,2,64,384]{3,2,1,0:T(8,128)(2,1)S(1)}, u32[]{:S(2)}, u32[]{:S(2)}) async-start(bf16[16,2,64,384]{3,2,1,0:T(8,128)(2,1)} %copy-done.9), calls=%async_computation.5 | async-start | bytes 3145728 | tf_op jit(solution)/shard_map/all_to_all | solution.py:506
  108.6 6.7 %copy-start.14 = (s32[16,56]{1,0:T(8,128)S(1)}, s32[16,56]{1,0:T(8,128)}, u32[]{:S(2)}) copy-start(s32[16,56]{1,0:T(8,128)} %piv_ref.5) | copy-start | bytes 10756
  108.6 29.3 %all-to-all-start.7 = ((bf16[16,2,64,384]{3,2,1,0:T(8,128)(2,1)}), bf16[16,2,64,384]{3,2,1,0:T(8,128)(2,1)S(1)}, u32[]{:S(2)}, u32[]{:S(2)}) async-start(bf16[16,2,64,384]{3,2,1,0:T(8,128)(2,1)} %copy-done.5), calls=%async_computation.7 | async-start | bytes 3145728 | tf_op jit(solution)/shard_map/all_to_all | solution.py:506
  115.3 1.1 copy-start.3
  121.4 1.1 copy-start.8
  122.6 0.7 copy-start.18
  137.9 28.0 %all-to-all-start.2 = ((f32[16,64,384]{2,1,0:T(8,128)}), f32[16,64,384]{2,1,0:T(8,128)}, u32[]{:S(2)}, u32[]{:S(2)}) async-start(f32[16,64,384]{2,1,0:T(8,128)} %copy-done.8), calls=%async_computation.2 | async-start | bytes 3145728 | tf_op jit(solution)/shard_map/all_to_all | solution.py:506
  144.4 1.4 copy-start
  146.9 1.1 copy-start.1
  165.9 42.3 %all-to-all-start.4 = ((bf16[16,2,64,384]{3,2,1,0:T(8,128)(2,1)}), bf16[16,2,64,384]{3,2,1,0:T(8,128)(2,1)}, u32[]{:S(2)}, u32[]{:S(2)}) async-start(bf16[16,2,64,384]{3,2,1,0:T(8,128)(2,1)} %copy-done.1), calls=%async_computation.4 | async-start | bytes 3145728 | tf_op jit(solution)/shard_map/all_to_all | solution.py:506
  171.5 1.1 copy-start.2
  208.2 42.6 %all-to-all-start.6 = ((bf16[16,2,64,384]{3,2,1,0:T(8,128)(2,1)}), bf16[16,2,64,384]{3,2,1,0:T(8,128)(2,1)S(1)}, u32[]{:S(2)}, u32[]{:S(2)}) async-start(bf16[16,2,64,384]{3,2,1,0:T(8,128)(2,1)} %copy-done.2), calls=%async_computation.6 | async-start | bytes 3145728 | tf_op jit(solution)/shard_map/all_to_all | solution.py:506
  215.3 40.4 %copy-start.19 = (f32[64,1024]{1,0:T(8,128)S(1)}, f32[64,1024]{1,0:T(8,128)}, u32[]{:S(2)}) copy-start(f32[64,1024]{1,0:T(8,128)} %copy-done.18) | copy-start | bytes 786436
  250.8 144.1 %all-to-all-start.8 = ((bf16[16,2,64,384]{3,2,1,0:T(8,128)(2,1)}), bf16[16,2,64,384]{3,2,1,0:T(8,128)(2,1)S(1)}, u32[]{:S(2)}, u32[]{:S(2)}) async-start(bf16[16,2,64,384]{3,2,1,0:T(8,128)(2,1)} %sort_trail.5), calls=%async_computation.8 | async-start | bytes 3145728 | tf_op jit(solution)/shard_map/all_to_all | solution.py:506
  255.6 1.1 copy-start.17
  390.1 1.1 copy-start.6
  391.2 0.9 copy-start.10
  392.1 0.8 copy-start.12
  394.9 1.1 copy-start.11
  396.0 18.0 %copy-start.7 = (f32[1024,384]{1,0:T(8,128)S(1)}, f32[1024,384]{1,0:T(8,128)}, u32[]{:S(2)}) copy-start(f32[1024,384]{1,0:T(8,128)} %copy-done.6) | copy-start | bytes 4718596

commit v3 on v2

v3 whole, which is shorter than its diff:
```python
import functools

import jax
import jax.numpy as jnp
from jax import lax
from jax.experimental import pallas as pl
from jax.experimental.pallas import tpu as pltpu
from jax.sharding import PartitionSpec as P

N = 1024
NB = 128
PC = 384
WT = N + PC
SLOTS = 56
KB = 24
KIDS = 32
F32 = jnp.float32
BF = jnp.bfloat16
MESH = pl.DeviceIdType.MESH


def vm():
    return pl.BlockSpec(memory_space=pltpu.VMEM)


def sm():
    return pl.BlockSpec(memory_space=pltpu.SMEM)


def split(x):
    hi = x.astype(BF)
    return hi, (x - hi.astype(F32)).astype(BF)


def dg(a, b, ca, cb):
    return lax.dot_general(a, b, (((ca,), (cb,)), ((), ())), preferred_element_type=F32)


def kid_order_table(parent_ref, order, count):
    for p in range(KIDS // 2):
        count[p] = 0
    for c in range(KIDS):
        p = parent_ref[c]
        n = count[p]
        order[2 * p + n] = c
        count[p] = n + 1


def slot_table(child, parent, map_ref, piv_ref, tab, slots, base):
    for v in range(SLOTS):
        tab[v] = -1
    for a in range(KB):
        tab[map_ref[child, a]] = a
    for s in range(SLOTS):
        slots[base + s] = tab[piv_ref[parent, s]]


def own_slots(parent_ref, map_ref, piv_ref, tab, slots, order, count):
    f = lax.axis_index("front")
    kid_order_table(parent_ref, order, count)
    for t in range(2):
        slot_table(order[2 * f + t], f, map_ref, piv_ref, tab, slots, t * SLOTS)


def pack_kernel(
    x_ref, map_ref, parent_ref, piv_ref,
    pan_ref, t0_ref, t1_ref, t2_ref, order_ref, src_ref, odd_ref, front_ref, unit_ref, has_ref,
    tab, slots, count,
):
    g = lax.axis_index("grid")
    for k in range(2):
        c = 2 * g + k
        slot_table(c, parent_ref[c], map_ref, piv_ref, tab, slots, k * SLOTS)
    own_slots(parent_ref, map_ref, piv_ref, tab, front_ref, order_ref, count)
    for c in range(KIDS):
        src_ref[c] = order_ref[c] // 2
        odd_ref[c] = (order_ref[c] % 2).astype(F32)

    def units(s, carry):
        a = front_ref[s]
        for v in range(2):
            unit_ref[2 * s + v] = 2 * jnp.maximum(a, 0) + v
        has_ref[s] = (a >= 0).astype(F32)
        return carry

    lax.fori_loop(0, 2 * SLOTS, units, 0)
    lane = lax.broadcasted_iota(jnp.int32, (192, NB), 1)

    def block(k, slot):
        a = slots[k * SLOTS + slot]
        off = pl.multiple_of(jnp.maximum(a, 0) * NB, NB)
        x = x_ref[k, :, pl.ds(off, NB)]
        return jnp.where(a >= 0, x, jnp.zeros_like(x))

    def panel(j, carry):
        x0 = block(0, j).astype(F32)
        x1 = block(1, j).astype(F32)
        r0 = pltpu.roll(x0, 64, 1)
        r1 = pltpu.roll(x1, 64, 1)
        pan_ref[2 * j] = jnp.where(lane < 64, x0, r1).astype(BF)
        pan_ref[2 * j + 1] = jnp.where(lane < 64, r0, x1).astype(BF)
        return carry

    lax.fori_loop(0, 8, panel, 0)

    def trail(m, carry):
        for k in range(2):
            for i in range(3):
                x = block(k, 8 + 3 * m + i)
                for s, t_ref in enumerate((t0_ref, t1_ref, t2_ref)):
                    t_ref[m, k, :, i * NB : (i + 1) * NB] = x[64 * s : 64 * s + 64]
        return carry

    lax.fori_loop(0, 16, trail, 0)


def pack(x, child_map, child_parent, pivot_order):
    t = jax.ShapeDtypeStruct((16, 2, 64, PC), BF)
    ints = lambda n: jax.ShapeDtypeStruct((n,), jnp.int32)
    floats = lambda n: jax.ShapeDtypeStruct((n,), F32)
    return pl.pallas_call(
        pack_kernel,
        out_shape=(
            jax.ShapeDtypeStruct((16, 192, NB), BF), t, t, t,
            ints(KIDS), ints(KIDS), floats(KIDS), ints(2 * SLOTS), ints(4 * SLOTS), floats(2 * SLOTS),
        ),
        in_specs=[vm(), sm(), sm(), sm()],
        out_specs=(vm(), vm(), vm(), vm(), sm(), sm(), sm(), sm(), sm(), sm()),
        scratch_shapes=[
            pltpu.SMEM((SLOTS,), jnp.int32),
            pltpu.SMEM((2 * SLOTS,), jnp.int32),
            pltpu.SMEM((KIDS // 2,), jnp.int32),
        ],
        compiler_params=pltpu.CompilerParams(vmem_limit_bytes=24 << 20),
        name="pack",
    )(x, child_map, child_parent, pivot_order)


def factor_block(m_ref, inv_ref, hook):
    rid = lax.broadcasted_iota(jnp.int32, (8, 1), 0)
    rows = [m_ref[8 * r : 8 * r + 8, :] for r in range(16)]
    for q in range(16):
        if q == 8:
            hook()
        c0 = 8 * q
        rb = [jnp.broadcast_to(rows[q][s : s + 1, :], (8, 2 * NB)) for s in range(8)]
        e = [
            [
                jnp.broadcast_to(rb[s][:, c0 + t : c0 + t + 1], (8, NB)) if t >= s else None
                for t in range(8)
            ]
            for s in range(8)
        ]
        inv = [None] * 8
        for t in range(8):
            inv[t] = 1.0 / e[t][t]
            for s in range(t + 1, 8):
                m = e[t][s] * inv[t]
                for u in range(s, 8):
                    e[s][u] = e[s][u] - m * e[t][u]
                rb[s] = rb[s] - jnp.concatenate([m, m], 1) * rb[t]
        new, iv = rb[7], inv[7]
        for s in range(6, -1, -1):
            new = jnp.where(rid == s, rb[s], new)
            iv = jnp.where(rid == s, inv[s], iv)
        m_ref[c0 : c0 + 8, :] = new
        inv_ref[c0 : c0 + 8, :] = iv
        if q < 15:
            cols = jnp.transpose(new[:, :NB] * iv)
            for r in range(q + 1, 16):
                p = [cols[8 * r : 8 * r + 8, t : t + 1] * rb[t] for t in range(8)]
                rows[r] = rows[r] - (
                    ((p[0] + p[1]) + (p[2] + p[3])) + ((p[4] + p[5]) + (p[6] + p[7]))
                )


class Gather:
    def __init__(self, own, out, send, recv, rows):
        self.own, self.out, self.send, self.recv, self.half = own, out, send, recv, rows // 2
        self.f = lax.axis_index("front")
        g = lax.axis_index("grid")
        self.x, self.y = g // 4, g % 4

    def dev(self, axis, d):
        if axis == 0:
            return (self.f, lax.rem(self.x + d, 4) * 4 + self.y)
        return (self.f, self.x * 4 + lax.rem(self.y + d, 4))

    def at(self, axis, d, r0, rn):
        x, y = self.x, self.y
        if axis == 0:
            x = lax.rem(x + d, 4)
        else:
            y = lax.rem(y + d, 4)
        return self.out.at[x, y, pl.ds(r0, rn), :]

    def line(self, axis, d, r0, rn):
        if axis == 0:
            return self.out.at[lax.rem(self.x + d, 4), :, pl.ds(r0, rn), :]
        return self.out.at[:, lax.rem(self.y + d, 4), pl.ds(r0, rn), :]

    def copy(self, src, dst, sem, axis, d):
        return pltpu.make_async_remote_copy(
            src_ref=src,
            dst_ref=dst,
            send_sem=self.send.at[sem],
            recv_sem=self.recv.at[sem],
            device_id=self.dev(axis, d),
            device_id_type=MESH,
        )

    def stage(self, n):
        h = self.half
        q = h // 2
        out = []
        for axis in range(2):
            r0 = axis * h
            other = 1 - axis
            b = axis * 8
            if n == 0:
                src = self.own.at[pl.ds(r0, h), :]
                for i, d in enumerate((1, 3, 2)):
                    out.append(self.copy(src, self.at(axis, 0, r0, h), b + i, axis, d))
            elif n == 1:
                a = self.line(other, 0, r0, h)
                out.append(self.copy(a, a, b + 3, other, 1))
                out.append(self.copy(a, a, b + 4, other, 3))
            else:
                a = self.line(other, 3, r0, q)
                out.append(self.copy(a, a, b + 5, other, 1))
                a = self.line(other, 1, r0 + q, q)
                out.append(self.copy(a, a, b + 6, other, 3))
        return out

    def start(self, n):
        for c in self.stage(n):
            c.start()

    def wait_recv(self, n):
        for c in self.stage(n):
            c.wait_recv()

    def wait_send(self):
        for n in range(3):
            for c in self.stage(n):
                c.wait_send()


class Swap:
    def __init__(self, axis, src, dst, send, recv, local):
        f, g = lax.axis_index("front"), lax.axis_index("grid")
        self.axis, self.f, self.g = axis, f, g
        self.me = g if axis == "grid" else f
        self.src, self.dst, self.send, self.recv, self.local = src, dst, send, recv, local

    def copy(self, i):
        if self.axis == "grid":
            to = lax.rem(self.g // 4 + i // 4, 4) * 4 + lax.rem(self.g % 4 + i % 4, 4)
            dev = (self.f, to)
        else:
            to = lax.rem(self.f // 2 + i // 2, 8) * 2 + lax.rem(self.f % 2 + i % 2, 2)
            dev = (to, self.g)
        return pltpu.make_async_remote_copy(
            src_ref=self.src.at[to],
            dst_ref=self.dst(self.me),
            send_sem=self.send.at[i],
            recv_sem=self.recv.at[i],
            device_id=dev,
            device_id_type=MESH,
        )

    def keep(self):
        return pltpu.make_async_copy(self.src.at[self.me], self.dst(self.me), self.local)

    def start(self):
        def one(i, c):
            self.copy(i).start()
            return c

        lax.fori_loop(1, 16, one, 0)
        self.keep().start()

    def wait_recv(self):
        def one(i, c):
            self.copy(i).wait_recv()
            return c

        lax.fori_loop(1, 16, one, 0)
        self.keep().wait()

    def wait_send(self):
        def one(i, c):
            self.copy(i).wait_send()
            return c

        lax.fori_loop(1, 16, one, 0)


def main_kernel(
    ps1, a0, a1, a2, od_ref, or_ref, order, src_tab, odd, unit, has,
    ud_ref, ur_ref, s_ref, sg_ref, o0_ref, o1_ref, o2_ref,
    pr1, ps2, pr2, b0, b1, b2, c0, c1, c2, dsnd, psnd, prcv,
    w, m_ref, inv_ref, uh, ul, st, dall,
    asend, arecv, dsend, drecv, ssend, srecv, lsem, ksem,
):
    f = lax.axis_index("front")
    g = lax.axis_index("grid")
    x, y = g // 4, g % 4
    barrier = pltpu.get_barrier_semaphore()

    def greet(i, c):
        to = lax.rem(g + i, 16)
        pl.semaphore_signal(barrier, inc=1, device_id=(f, to), device_id_type=MESH)
        to = lax.rem(f + i, 16)
        pl.semaphore_signal(barrier, inc=1, device_id=(to, g), device_id_type=MESH)
        return c

    lax.fori_loop(1, 16, greet, 0)

    def swap(n, axis, src, dst):
        return Swap(axis, src, dst, asend.at[n], arecv.at[n], ksem.at[n])

    lane = lax.broadcasted_iota(jnp.int32, (192, NB), 1)

    panel1 = swap(0, "grid", ps1, lambda me: pr1.at[me])
    panel2 = swap(1, "front", ps2, lambda me: pr2.at[pl.ds(3 * me, 3)])
    pswap = swap(2, "grid", psnd, lambda me: prcv.at[pl.ds(64 * me, 64), :])

    def trail1(s):
        dst = (b0, b1, b2)[s]
        return swap(3 + s, "grid", (a0, a1, a2)[s], lambda me: dst.at[pl.ds(2 * me, 2)])

    def trail2(s):
        dst = (o0_ref, o1_ref, o2_ref)[s]
        return swap(6 + s, "front", (c0, c1, c2)[s], lambda me: dst.at[me])

    pl.semaphore_wait(barrier, 30)
    panel1.start()

    trail1(0).start()
    trail1(1).start()
    panel1.wait_recv()

    def sort_panel(p, carry):
        x0 = pr1[src_tab[2 * p]].astype(F32)
        x1 = pr1[src_tab[2 * p + 1]].astype(F32)
        m0 = odd[2 * p]
        m1 = odd[2 * p + 1]
        x0 = x0 * (1.0 - m0) + pltpu.roll(x0, 64, 1) * m0
        x1 = x1 * m1 + pltpu.roll(x1, 64, 1) * (1.0 - m1)
        z = jnp.where(lane < 64, x0, x1).astype(BF)
        for v in range(3):
            ps2[p, v] = z[64 * v : 64 * v + 64]
        return carry

    lax.fori_loop(0, 16, sort_panel, 0)
    panel2.start()

    def sort_trail(s):
        trail1(s).wait_recv()
        src, dst = (b0, b1, b2)[s], (c0, c1, c2)[s]

        def one(p, carry):
            for t in range(2):
                dst[p, t] = src[order[2 * p + t]]
            return carry

        lax.fori_loop(0, 16, one, 0)
        trail2(s).start()

    sort_trail(0)
    panel2.wait_recv()

    def pivot_rows(slot):
        halves = []
        for v in range(2):
            total = jnp.zeros((64, NB), F32)
            for t in range(2):
                z = pr2[unit[2 * (t * SLOTS + slot) + v]].astype(F32)
                if t == 1:
                    z = pltpu.roll(z, 64, 1)
                total = total + z * has[t * SLOTS + slot]
            halves.append(total)
        return jnp.transpose(jnp.concatenate(halves, 0))[:64]

    for j in range(8):
        od = jnp.transpose(od_ref[0, j * NB : (j + 1) * NB, :].astype(F32))
        dsnd[:, j * NB : (j + 1) * NB] = pivot_rows(j) + od
    gd = Gather(dsnd, dall, dsend, drecv, 64)
    gd.start(0)
    dall[x, y] = dsnd[...]

    def rest(m, carry):
        for i in range(3):
            psnd[m, :, i * NB : (i + 1) * NB] = pivot_rows(8 + 3 * m + i)
        return carry

    lax.fori_loop(0, 16, rest, 0)
    for n in range(2):
        gd.wait_recv(n)
        gd.start(n + 1)
    pswap.start()
    trail1(2).start()
    sort_trail(1)
    gd.wait_recv(2)
    for i in range(16):
        w[64 * i : 64 * i + 64, :N] = dall[i // 4, i % 4]
    eye = (
        lax.broadcasted_iota(jnp.int32, (NB, NB), 0) == lax.broadcasted_iota(jnp.int32, (NB, NB), 1)
    ).astype(F32)

    def gs(k):
        return Gather(st.at[k], sg_ref.at[k], ssend.at[k], srecv.at[k], PC)

    def local(k):
        return pltpu.make_async_copy(st.at[k], sg_ref.at[k, x, y], lsem.at[k])

    def move(k, n):
        c = gs(k)
        c.wait_recv(n - 1)
        if n == 1:
            local(k).wait()
        c.start(n)

    def step(k, carry):
        r0 = pl.multiple_of(k * NB, NB)
        m_ref[:, :NB] = w[pl.ds(r0, NB), pl.ds(r0, NB)]
        m_ref[:, NB:] = eye

        def hook():
            @pl.when(k >= 1)
            def _():
                move(k - 1, 1)

        factor_block(m_ref, inv_ref, hook)

        @pl.when(k == 0)
        def _():
            pswap.wait_recv()
            w[:, N:] = prcv[...] + or_ref[0].astype(F32)

        @pl.when(k == 2)
        def _():
            sort_trail(2)

        lh, ll = split(m_ref[:, NB:])
        ah, al = split(w[pl.ds(r0, NB), :])
        u = dg(lh, ah, 1, 0) + (dg(lh, al, 1, 0) + dg(ll, ah, 1, 0))
        w[pl.ds(r0, NB), :] = u
        h, l = split(u)
        uh[...] = h
        ul[...] = l
        iv = inv_ref[...]
        top = u[:, N:]
        ur_ref[pl.ds(r0, NB), :] = top
        rs = jnp.sqrt(iv)
        solved = top * jnp.concatenate([rs] * 3, 1)
        s_ref[pl.ds(r0, NB), :] = solved.astype(BF)
        st[k] = jnp.transpose(solved).astype(BF)
        gs(k).start(0)
        local(k).start()

        def upd(i, c):
            i0 = pl.multiple_of(i * NB, NB)
            xh, xl = split((uh[:, pl.ds(i0, NB)].astype(F32) + ul[:, pl.ds(i0, NB)].astype(F32)) * iv)
            d = dg(xh, uh[...], 0, 0) + (dg(xh, ul[...], 0, 0) + dg(xl, uh[...], 0, 0))
            w[pl.ds(i0, NB), :] = w[pl.ds(i0, NB), :] - d
            return c

        lax.fori_loop(k + 1, N // NB, upd, 0)

        @pl.when(k >= 1)
        def _():
            move(k - 1, 2)

        return carry

    last = N // NB - 1
    lax.fori_loop(0, N // NB, step, 0)
    move(last, 1)
    blk = pl.multiple_of((g // 2) * NB, NB)
    own = w[:, pl.ds(blk, NB)]
    own = jnp.where(g % 2 == 1, own[:, 64:], own[:, :64])
    col = 64 * g + lax.broadcasted_iota(jnp.int32, (N, 64), 1)
    ud_ref[...] = jnp.where(lax.broadcasted_iota(jnp.int32, (N, 64), 0) <= col, own, 0.0)
    move(last, 2)
    for s in range(3):
        trail1(s).wait_send()
        trail2(s).wait_send()
        trail2(s).wait_recv()
    for e in (panel1, panel2, pswap):
        e.wait_send()
    gd.wait_send()

    def finish(k, carry):
        c = gs(k)
        c.wait_recv(2)
        c.wait_send()
        return carry

    lax.fori_loop(0, N // NB, finish, 0)


def main_call(ps1, a0, a1, a2, orig_diag, orig_rows, *tables):
    steps = N // NB
    hbm = pl.BlockSpec(memory_space=pl.ANY)
    out = jax.ShapeDtypeStruct((16, 2, 64, PC), BF)
    panel = pltpu.VMEM((16, 192, NB), BF)
    send = pltpu.VMEM((16, 2, 64, PC), BF)
    recv = pltpu.VMEM((KIDS, 64, PC), BF)
    sems = pltpu.SemaphoreType.DMA
    return pl.pallas_call(
        main_kernel,
        out_shape=(
            jax.ShapeDtypeStruct((N, 64), F32),
            jax.ShapeDtypeStruct((N, PC), F32),
            jax.ShapeDtypeStruct((N, PC), BF),
            jax.ShapeDtypeStruct((steps, 4, 4, PC, NB), BF),
            out, out, out,
        ),
        in_specs=[hbm, hbm, hbm, hbm, vm(), vm(), sm(), sm(), sm(), sm(), sm()],
        out_specs=(vm(), vm(), vm(), hbm, hbm, hbm, hbm),
        scratch_shapes=[
            panel, pltpu.VMEM((16, 3, 64, NB), BF), pltpu.VMEM((48, 64, NB), BF),
            recv, recv, recv, send, send, send,
            pltpu.VMEM((64, N), F32),
            pltpu.VMEM((16, 64, PC), F32),
            pltpu.VMEM((N, PC), F32),
            pltpu.VMEM((N, WT), F32),
            pltpu.VMEM((NB, 2 * NB), F32),
            pltpu.VMEM((NB, NB), F32),
            pltpu.VMEM((NB, WT), BF),
            pltpu.VMEM((NB, WT), BF),
            pltpu.VMEM((steps, PC, NB), BF),
            pltpu.VMEM((4, 4, 64, N), F32),
            sems((9, 16)), sems((9, 16)), sems((16,)), sems((16,)),
            sems((steps, 16)), sems((steps, 16)), sems((steps,)), sems((9,)),
        ],
        compiler_params=pltpu.CompilerParams(
            vmem_limit_bytes=56 << 20, collective_id=0, has_side_effects=True
        ),
        name="assemble_factor_gather",
    )(ps1, a0, a1, a2, orig_diag, orig_rows, *tables)


def schur_kernel(
    sg_ref, s_ref, t0_ref, t1_ref, t2_ref, slots, o_ref
):
    m = pl.program_id(0)

    lhs = jnp.concatenate([sg_ref[k, 0] for k in range(N // NB)], 1)
    prod = dg(lhs, s_ref[...], 1, 0)
    for i in range(3):
        for v in range(2):
            total = -prod[i * NB + v * 64 : i * NB + v * 64 + 64]
            for t in range(2):
                a = slots[t * SLOTS + 8 + 3 * m + i]
                u = 2 * jnp.maximum(a, 0) + v
                s = u % 3
                x = jnp.where(
                    s == 0, t0_ref[u // 3, t], jnp.where(s == 1, t1_ref[u // 3, t], t2_ref[u // 3, t])
                )
                total = total + jnp.where(a >= 0, x.astype(F32), 0.0)
            o_ref[0, i * NB + v * 64 : i * NB + v * 64 + 64, :] = total.astype(BF)


def schur_call(sg, s, t0, t1, t2, front):
    steps = N // NB
    return pl.pallas_call(
        schur_kernel,
        out_shape=jax.ShapeDtypeStruct((1, 16 * PC, PC), BF),
        grid=(16,),
        in_specs=[
            pl.BlockSpec((steps, 1, PC, NB), lambda m: (0, m, 0, 0)),
            vm(), vm(), vm(), vm(), sm(),
        ],
        out_specs=pl.BlockSpec((1, PC, PC), lambda m: (0, m, 0)),
        compiler_params=pltpu.CompilerParams(vmem_limit_bytes=40 << 20),
        name="schur",
    )(sg.reshape(steps, 16, PC, NB), s, t0, t1, t2, front)


def shards(child_blocks, orig_diag, orig_rows, child_map, child_parent, pivot_order):
    panel, a0, a1, a2, order, src, odd, front, unit, has = pack(
        child_blocks, child_map, child_parent, pivot_order
    )
    upper_diag, upper_rows, s, sg, *trail = main_call(
        panel, a0, a1, a2, orig_diag, orig_rows, order, src, odd, unit, has
    )
    schur = schur_call(sg, s, *trail, front)
    return upper_diag[None], upper_rows[None], schur


def solution(mesh):
    return jax.shard_map(
        shards,
        mesh=mesh,
        in_specs=(
            P("grid", "front", None),
            P("front", None, "grid"),
            P("front", None, "grid"),
            P(),
            P(),
            P(),
        ),
        out_specs=(P("front", None, "grid"), P("front", None, "grid"), P("front", None, "grid")),
        check_vma=False,
    )
```

time: 417 us -> 266 us (0.64)
  waiting for transfers between devices: 121 us -> 0 us
  Pallas kernels: 167 us -> 244 us
  blocking collectives: 75.3 us -> 0 us
  starting transfers between devices: 32 us -> 0 us
    all_to_all x6 -> x0, waiting for transfers between devices: 121 us -> none  [exchange(): return lax.all_to_all(x, axis, split_axis=0, concat_axis=0, tiled=True)]
    pallas_call x6 -> x1, Pallas kernels: 145 us -> 221 us  [main_call(): pl.pallas_call(main_kernel, out_shape=(jax.ShapeDtypeStruct((N, 64), F32)...]
    all_to_all x3 -> x0, blocking collectives: 75.3 us -> none  [exchange(): return lax.all_to_all(x, axis, split_axis=0, concat_axis=0, tiled=True)]
    all_to_all x6 -> x0, starting transfers between devices: 32 us -> none  [exchange(): return lax.all_to_all(x, axis, split_axis=0, concat_axis=0, tiled=True)]
    unnamed x44 -> x38, local copies, waits for them, and re-layouts: 19.7 us -> 21 us
  transfers between devices with their start and end apart: 6 -> 0, of which waited for: 5 -> 0; matrix products, arithmetic and copies ran while one was open for 1% -> 0% of each run, Pallas kernels for 35% -> 0%
where the time goes in v3:
time: 266 us; the launch traced here: 265 us
  Pallas kernels  244 us (92%)
  local copies, waits for them, and re-layouts  21 us (8%)
    pallas_call x1, Pallas kernels, main_call(): pl.pallas_call(main_kernel, out_shape=(jax.ShapeDtypeStruct((N, 64), F32)...  221 us
    unnamed x38, local copies, waits for them, and re-layouts  21 us
    pallas_call x1, Pallas kernels, schur_call(): pl.pallas_call(schur_kernel, out_shape=jax.ShapeDtypeStruct((1, 16 * PC,...  17.1 us
    pallas_call x1, Pallas kernels, pack(): pl.pallas_call(pack_kernel, out_shape=(jax.ShapeDtypeStruct((16, 192, NB)...  5.58 us

profile of v3, /device:TPU:2, one launch (start us, length us, event | category | flops | bytes accessed | tf_op | source)
XLA Modules:
  0.0 265.3 jit_solution(15049056118143093183)
XLA Ops:
  0.6 0.8 copy.9.map_ref
  1.4 1.7 copy.10.od_ref
  3.2 0.0 copy-start
  3.2 1.7 copy-done
  4.8 0.0 copy-start.9
  4.8 0.7 copy-done.9
  5.5 0.0 copy-start.15
  5.5 0.7 copy-done.15
  6.2 5.6 %pack.1 = (bf16[16,192,128]{2,1,0:T(8,128)(2,1)S(1)}, bf16[16,2,64,384]{3,2,1,0:T(8,128)(2,1)S(1)}, bf16[16,2,64,384]{3,2,1,0:T(8,128)(2,1)S(1)}, bf16[16,2,64,3...) custom-call(bf16[2,192,3072]{2,1,0:T(8,128)(2,1)S(1)} %copy-done, ...), custom_call_target="tpu_custom_call" | custom-call | tf_op jit(solution)/shard_map/pack/pallas_call | solution.py:121
  11.8 0.0 copy-start.4
  11.8 1.1 copy-done.4
  12.9 0.0 copy-start.5
  12.9 1.1 copy-done.5
  14.1 0.0 copy-start.6
  14.1 1.2 copy-done.6
  15.2 0.0 copy-start.8
  15.2 0.9 copy-done.8
  16.1 0.0 copy-start.10
  16.1 0.5 copy-done.10
  16.6 0.0 copy-start.11
  16.6 0.6 copy-done.11
  17.2 0.0 copy-start.12
  17.2 0.5 copy-done.12
  17.7 0.0 copy-start.13
  17.7 0.5 copy-done.13
  18.2 0.0 copy-start.14
  18.2 0.6 copy-done.14
  18.8 220.9 %assemble_factor_gather.1 = (f32[1024,64]{1,0:T(8,128)}, f32[1024,384]{1,0:T(8,128)}, bf16[1024,384]{1,0:T(8,128)(2,1)}, bf16[8,4,4,384,128]{4,3,2,1,0:T(8,128)(...) custom-call(bf16[16,192,128]{2,1,0:T(8,128)(2,1)} %copy-done.8, ...), custom_call_target="tpu_custom_call" | custom-call | tf_op jit(solution)/shard_map/assemble_factor_gather/pallas_call | solution.py:512
  239.7 1.9 copy.11
  241.7 0.0 copy-start.1
  241.7 1.4 copy-done.1
  243.1 0.0 copy-start.2
  243.1 1.4 copy-done.2
  244.5 0.0 copy-start.3
  244.5 1.4 copy-done.3
  245.9 0.0 copy-start.7
  245.9 1.1 copy-done.7
  247.0 0.0 copy-start.16
  247.0 17.1 %schur.1 = bf16[1,6144,384]{2,1,0:T(8,128)(2,1)} custom-call(bf16[8,16,384,128]{3,2,1,0:T(8,128)(2,1)} %bitcast.3, bf16[1024,384]{1,0:T(8,128)(2,1)S(1)} %copy-done.7, bf16[16,2,64,384]{3,2,1,0:T(8,128)(2,1)S(1)} %copy-done.1, bf16[16,2,64,384]{3,2,1,0:T(8,128)(2,1)S(1)} %copy-done.2, bf16[16,2,64,384]{3,2,1,0:T(8,128)(2,1)S(1)} %copy-done.3, ...), custom_call_target="tpu_custom_call" | custom-call | tf_op jit(solution)/shard_map/schur/pallas_call | solution.py:569
  264.2 0.0 copy-done.16
  264.2 1.1 copy.13
Async XLA Ops:
  3.2 1.7 copy-start
  4.8 0.7 copy-start.9
  5.5 0.7 copy-start.15
  11.8 1.1 copy-start.4
  12.9 1.1 copy-start.5
  14.1 1.2 copy-start.6
  15.2 0.9 copy-start.8
  16.1 0.5 copy-start.10
  16.6 0.6 copy-start.11
  17.2 0.5 copy-start.12
  17.7 0.5 copy-start.13
  18.2 0.6 copy-start.14
  241.7 1.4 copy-start.1
  243.1 1.4 copy-start.2
  244.5 1.4 copy-start.3
  245.9 1.1 copy-start.7
  247.0 17.1 %copy-start.16 = (f32[1024,384]{1,0:T(8,128)S(1)}, f32[1024,384]{1,0:T(8,128)}, u32[]{:S(2)}) copy-start(f32[1024,384]{1,0:T(8,128)} %get-tuple-element.30) | copy-start | bytes 4718596

commit v4 on v3

--- a/solution.py
+++ b/solution.py
@@ -14,6 +14,14 @@
 SLOTS = 56
 KB = 24
 KIDS = 32
+ORDER = 0
+SOURCE = ORDER + KIDS
+UNIT = SOURCE + KIDS
+FRONT = UNIT + 4 * SLOTS
+INTS = FRONT + 2 * SLOTS
+HAS = KIDS
+FLOATS = HAS + 2 * SLOTS
+PW = 5 * NB
 F32 = jnp.float32
 BF = jnp.bfloat16
 MESH = pl.DeviceIdType.MESH
@@ -64,8 +72,8 @@
 
 def pack_kernel(
     x_ref, map_ref, parent_ref, piv_ref,
-    pan_ref, t0_ref, t1_ref, t2_ref, order_ref, src_ref, odd_ref, front_ref, unit_ref, has_ref,
-    tab, slots, count,
+    pan_ref, t0_ref, t1_ref, t2_ref, int_ref, float_ref,
+    tab, slots, count, order_ref, front_ref,
 ):
     g = lax.axis_index("grid")
     for k in range(2):
@@ -73,14 +81,16 @@
         slot_table(c, parent_ref[c], map_ref, piv_ref, tab, slots, k * SLOTS)
     own_slots(parent_ref, map_ref, piv_ref, tab, front_ref, order_ref, count)
     for c in range(KIDS):
-        src_ref[c] = order_ref[c] // 2
-        odd_ref[c] = (order_ref[c] % 2).astype(F32)
+        int_ref[ORDER + c] = order_ref[c]
+        int_ref[SOURCE + c] = order_ref[c] // 2
+        float_ref[c] = (order_ref[c] % 2).astype(F32)
 
     def units(s, carry):
         a = front_ref[s]
         for v in range(2):
-            unit_ref[2 * s + v] = 2 * jnp.maximum(a, 0) + v
-        has_ref[s] = (a >= 0).astype(F32)
+            int_ref[UNIT + 2 * s + v] = 2 * jnp.maximum(a, 0) + v
+        int_ref[FRONT + s] = a
+        float_ref[HAS + s] = (a >= 0).astype(F32)
         return carry
 
     lax.fori_loop(0, 2 * SLOTS, units, 0)
@@ -116,20 +126,20 @@
 
 def pack(x, child_map, child_parent, pivot_order):
     t = jax.ShapeDtypeStruct((16, 2, 64, PC), BF)
-    ints = lambda n: jax.ShapeDtypeStruct((n,), jnp.int32)
-    floats = lambda n: jax.ShapeDtypeStruct((n,), F32)
     return pl.pallas_call(
         pack_kernel,
         out_shape=(
             jax.ShapeDtypeStruct((16, 192, NB), BF), t, t, t,
-            ints(KIDS), ints(KIDS), floats(KIDS), ints(2 * SLOTS), ints(4 * SLOTS), floats(2 * SLOTS),
+            jax.ShapeDtypeStruct((INTS,), jnp.int32), jax.ShapeDtypeStruct((FLOATS,), F32),
         ),
         in_specs=[vm(), sm(), sm(), sm()],
-        out_specs=(vm(), vm(), vm(), vm(), sm(), sm(), sm(), sm(), sm(), sm()),
+        out_specs=(vm(), vm(), vm(), vm(), sm(), sm()),
         scratch_shapes=[
             pltpu.SMEM((SLOTS,), jnp.int32),
             pltpu.SMEM((2 * SLOTS,), jnp.int32),
             pltpu.SMEM((KIDS // 2,), jnp.int32),
+            pltpu.SMEM((KIDS,), jnp.int32),
+            pltpu.SMEM((2 * SLOTS,), jnp.int32),
         ],
         compiler_params=pltpu.CompilerParams(vmem_limit_bytes=24 << 20),
         name="pack",
@@ -297,7 +307,7 @@
 
 
 def main_kernel(
-    ps1, a0, a1, a2, od_ref, or_ref, order, src_tab, odd, unit, has,
+    ps1, a0, a1, a2, od_ref, or_ref, ints, floats,
     ud_ref, ur_ref, s_ref, sg_ref, o0_ref, o1_ref, o2_ref,
     pr1, ps2, pr2, b0, b1, b2, c0, c1, c2, dsnd, psnd, prcv,
     w, m_ref, inv_ref, uh, ul, st, dall,
@@ -342,10 +352,10 @@
     panel1.wait_recv()
 
     def sort_panel(p, carry):
-        x0 = pr1[src_tab[2 * p]].astype(F32)
-        x1 = pr1[src_tab[2 * p + 1]].astype(F32)
-        m0 = odd[2 * p]
-        m1 = odd[2 * p + 1]
+        x0 = pr1[ints[SOURCE + 2 * p]].astype(F32)
+        x1 = pr1[ints[SOURCE + 2 * p + 1]].astype(F32)
+        m0 = floats[2 * p]
+        m1 = floats[2 * p + 1]
         x0 = x0 * (1.0 - m0) + pltpu.roll(x0, 64, 1) * m0
         x1 = x1 * m1 + pltpu.roll(x1, 64, 1) * (1.0 - m1)
         z = jnp.where(lane < 64, x0, x1).astype(BF)
@@ -362,7 +372,7 @@
 
         def one(p, carry):
             for t in range(2):
-                dst[p, t] = src[order[2 * p + t]]
+                dst[p, t] = src[ints[ORDER + 2 * p + t]]
             return carry
 
         lax.fori_loop(0, 16, one, 0)
@@ -376,16 +386,17 @@
         for v in range(2):
             total = jnp.zeros((64, NB), F32)
             for t in range(2):
-                z = pr2[unit[2 * (t * SLOTS + slot) + v]].astype(F32)
+                z = pr2[ints[UNIT + 2 * (t * SLOTS + slot) + v]].astype(F32)
                 if t == 1:
                     z = pltpu.roll(z, 64, 1)
-                total = total + z * has[t * SLOTS + slot]
+                total = total + z * floats[HAS + t * SLOTS + slot]
             halves.append(total)
         return jnp.transpose(jnp.concatenate(halves, 0))[:64]
 
-    for j in range(8):
-        od = jnp.transpose(od_ref[0, j * NB : (j + 1) * NB, :].astype(F32))
-        dsnd[:, j * NB : (j + 1) * NB] = pivot_rows(j) + od
+    for i in range(5):
+        j = lax.rem(g // 2 + i, 8)
+        od = od_ref[:, pl.ds(pl.multiple_of(j * NB, NB), NB)].astype(F32)
+        dsnd[:, i * NB : (i + 1) * NB] = pivot_rows(j) + od
     gd = Gather(dsnd, dall, dsend, drecv, 64)
     gd.start(0)
     dall[x, y] = dsnd[...]
@@ -403,8 +414,21 @@
     trail1(2).start()
     sort_trail(1)
     gd.wait_recv(2)
-    for i in range(16):
-        w[64 * i : 64 * i + 64, :N] = dall[i // 4, i % 4]
+
+    def cyclic(r, i):
+        return jnp.concatenate(
+            [dall[b // 4, b % 4, :, i * NB : (i + 1) * NB] for b in (2 * r, 2 * r + 1)], 0
+        )
+
+    for r in range(8):
+        for c in range(8):
+            if c < r:
+                z = jnp.zeros((NB, NB), F32)
+            elif c - r <= 4:
+                z = cyclic(r, c - r)
+            else:
+                z = jnp.transpose(cyclic(c, 8 - (c - r)))
+            w[r * NB : (r + 1) * NB, c * NB : (c + 1) * NB] = z
     eye = (
         lax.broadcasted_iota(jnp.int32, (NB, NB), 0) == lax.broadcasted_iota(jnp.int32, (NB, NB), 1)
     ).astype(F32)
@@ -479,10 +503,12 @@
     lax.fori_loop(0, N // NB, step, 0)
     move(last, 1)
     blk = pl.multiple_of((g // 2) * NB, NB)
-    own = w[:, pl.ds(blk, NB)]
-    own = jnp.where(g % 2 == 1, own[:, 64:], own[:, :64])
-    col = 64 * g + lax.broadcasted_iota(jnp.int32, (N, 64), 1)
-    ud_ref[...] = jnp.where(lax.broadcasted_iota(jnp.int32, (N, 64), 0) <= col, own, 0.0)
+    col = 64 * g + lax.broadcasted_iota(jnp.int32, (64, NB), 0)
+    for r in range(8):
+        own = jnp.transpose(w[r * NB : (r + 1) * NB, pl.ds(blk, NB)])
+        own = jnp.where(g % 2 == 1, own[64:], own[:64])
+        row = r * NB + lax.broadcasted_iota(jnp.int32, (64, NB), 1)
+        ud_ref[:, r * NB : (r + 1) * NB] = jnp.where(row <= col, own, 0.0)
     move(last, 2)
     for s in range(3):
         trail1(s).wait_send()
@@ -512,18 +538,18 @@
     return pl.pallas_call(
         main_kernel,
         out_shape=(
-            jax.ShapeDtypeStruct((N, 64), F32),
+            jax.ShapeDtypeStruct((64, N), F32),
             jax.ShapeDtypeStruct((N, PC), F32),
             jax.ShapeDtypeStruct((N, PC), BF),
             jax.ShapeDtypeStruct((steps, 4, 4, PC, NB), BF),
             out, out, out,
         ),
-        in_specs=[hbm, hbm, hbm, hbm, vm(), vm(), sm(), sm(), sm(), sm(), sm()],
-        out_specs=(vm(), vm(), vm(), hbm, hbm, hbm, hbm),
+        in_specs=[vm(), vm(), vm(), vm(), vm(), vm(), sm(), sm()],
+        out_specs=(vm(), vm(), vm(), hbm, vm(), vm(), vm()),
         scratch_shapes=[
             panel, pltpu.VMEM((16, 3, 64, NB), BF), pltpu.VMEM((48, 64, NB), BF),
             recv, recv, recv, send, send, send,
-            pltpu.VMEM((64, N), F32),
+            pltpu.VMEM((64, PW), F32),
             pltpu.VMEM((16, 64, PC), F32),
             pltpu.VMEM((N, PC), F32),
             pltpu.VMEM((N, WT), F32),
@@ -532,29 +558,30 @@
             pltpu.VMEM((NB, WT), BF),
             pltpu.VMEM((NB, WT), BF),
             pltpu.VMEM((steps, PC, NB), BF),
-            pltpu.VMEM((4, 4, 64, N), F32),
+            pltpu.VMEM((4, 4, 64, PW), F32),
             sems((9, 16)), sems((9, 16)), sems((16,)), sems((16,)),
             sems((steps, 16)), sems((steps, 16)), sems((steps,)), sems((9,)),
         ],
         compiler_params=pltpu.CompilerParams(
-            vmem_limit_bytes=56 << 20, collective_id=0, has_side_effects=True
+            vmem_limit_bytes=40 << 20, collective_id=0, has_side_effects=True
         ),
         name="assemble_factor_gather",
     )(ps1, a0, a1, a2, orig_diag, orig_rows, *tables)
 
 
 def schur_kernel(
-    sg_ref, s_ref, t0_ref, t1_ref, t2_ref, slots, o_ref
+    sg_ref, s_ref, t0_ref, t1_ref, t2_ref, ud_ref, ur_ref, slots, o_ref, udo_ref, uro_ref
 ):
     m = pl.program_id(0)
-
+    uro_ref[0] = ur_ref[...]
+    udo_ref[...] = ud_ref[...]
     lhs = jnp.concatenate([sg_ref[k, 0] for k in range(N // NB)], 1)
     prod = dg(lhs, s_ref[...], 1, 0)
     for i in range(3):
         for v in range(2):
             total = -prod[i * NB + v * 64 : i * NB + v * 64 + 64]
             for t in range(2):
-                a = slots[t * SLOTS + 8 + 3 * m + i]
+                a = slots[FRONT + t * SLOTS + 8 + 3 * m + i]
                 u = 2 * jnp.maximum(a, 0) + v
                 s = u % 3
                 x = jnp.where(
@@ -564,31 +591,40 @@
             o_ref[0, i * NB + v * 64 : i * NB + v * 64 + 64, :] = total.astype(BF)
 
 
-def schur_call(sg, s, t0, t1, t2, front):
+def schur_call(sg, s, t0, t1, t2, ud, ur, ints):
     steps = N // NB
     return pl.pallas_call(
         schur_kernel,
-        out_shape=jax.ShapeDtypeStruct((1, 16 * PC, PC), BF),
+        out_shape=(
+            jax.ShapeDtypeStruct((1, 16 * PC, PC), BF),
+            jax.ShapeDtypeStruct((64, N), F32),
+            jax.ShapeDtypeStruct((1, N, PC), F32),
+        ),
         grid=(16,),
         in_specs=[
             pl.BlockSpec((steps, 1, PC, NB), lambda m: (0, m, 0, 0)),
-            vm(), vm(), vm(), vm(), sm(),
+            vm(), vm(), vm(), vm(),
+            pl.BlockSpec((64, NB), lambda m: (0, m // 2)),
+            pl.BlockSpec((64, PC), lambda m: (m, 0)),
+            sm(),
         ],
-        out_specs=pl.BlockSpec((1, PC, PC), lambda m: (0, m, 0)),
-        compiler_params=pltpu.CompilerParams(vmem_limit_bytes=40 << 20),
+        out_specs=(
+            pl.BlockSpec((1, PC, PC), lambda m: (0, m, 0)),
+            pl.BlockSpec((64, NB), lambda m: (0, m // 2)),
+            pl.BlockSpec((1, 64, PC), lambda m: (0, m, 0)),
+        ),
+        compiler_params=pltpu.CompilerParams(vmem_limit_bytes=46 << 20),
         name="schur",
-    )(sg.reshape(steps, 16, PC, NB), s, t0, t1, t2, front)
+    )(sg.reshape(steps, 16, PC, NB), s, t0, t1, t2, ud, ur, ints)
 
 
 def shards(child_blocks, orig_diag, orig_rows, child_map, child_parent, pivot_order):
-    panel, a0, a1, a2, order, src, odd, front, unit, has = pack(
-        child_blocks, child_map, child_parent, pivot_order
+    panel, a0, a1, a2, ints, floats = pack(child_blocks, child_map, child_parent, pivot_order)
+    upper_diag, upper_rows, s, sg, *trail = main_call(
+        panel, a0, a1, a2, orig_diag[0].T, orig_rows, ints, floats
     )
-    upper_diag, upper_rows, s, sg, *trail = main_call(
-        panel, a0, a1, a2, orig_diag, orig_rows, order, src, odd, unit, has
-    )
-    schur = schur_call(sg, s, *trail, front)
-    return upper_diag[None], upper_rows[None], schur
+    schur, upper_diag, upper_rows = schur_call(sg, s, *trail, upper_diag, upper_rows, ints)
+    return upper_diag.T[None], upper_rows, schur
 
 
 def solution(mesh):

time: 266 us -> 235 us (0.88)
  local copies, waits for them, and re-layouts: 21 us -> 3.81 us
  Pallas kernels: 244 us -> 230 us
    unnamed x38 -> x11, local copies, waits for them, and re-layouts: 21 us -> 3.81 us
    pallas_call x2, Pallas kernels: 238 us -> 225 us  [the longest x1 208 us: main_call(): pl.pallas_call(main_kernel, out_shape=(jax.ShapeDtypeStruct((64, N), F32)...]
where the time goes in v4:
time: 235 us
  Pallas kernels  230 us (98%)
  local copies, waits for them, and re-layouts  3.81 us (2%)
    pallas_call x1, Pallas kernels, main_call(): pl.pallas_call(main_kernel, out_shape=(jax.ShapeDtypeStruct((64, N), F32)...  208 us
    pallas_call x1, Pallas kernels, schur_call(): pl.pallas_call(schur_kernel, out_shape=(jax.ShapeDtypeStruct((1, 16 * PC,...  17.1 us
    pallas_call x1, Pallas kernels, pack(): pl.pallas_call(pack_kernel, out_shape=(jax.ShapeDtypeStruct((16, 192, NB)...  5.69 us

profile of v4, /device:TPU:2, one launch (start us, length us, event | category | flops | bytes accessed | tf_op | source)
XLA Modules:
  0.0 234.9 jit_solution(13212687113799476761)
XLA Ops:
  0.6 0.8 copy.9.map_ref
  1.4 0.0 copy-start
  1.4 1.7 copy-done
  3.1 0.0 copy-start.3
  3.1 0.7 copy-done.3
  3.8 0.0 copy-start.4
  3.8 0.7 copy-done.4
  4.4 0.0 copy-start.1
  4.4 0.0 copy-start.2
  4.4 5.7 %pack.1 = (bf16[16,192,128]{2,1,0:T(8,128)(2,1)S(1)}, bf16[16,2,64,384]{3,2,1,0:T(8,128)(2,1)S(1)}, bf16[16,2,64,384]{3,2,1,0:T(8,128)(2,1)S(1)}, bf16[16,2,64,3...) custom-call(bf16[2,192,3072]{2,1,0:T(8,128)(2,1)S(1)} %copy-done, s32[32,24]{1,0:T(8,128)S(1)} %copy.9.map_ref, ...), custom_call_target="tpu_custom_call" | custom-call | tf_op jit(solution)/shard_map/pack/pallas_call | solution.py:129
  10.1 0.0 copy-done.1
  10.1 0.0 copy-done.2
  10.2 207.6 %assemble_factor_gather.1 = (f32[64,1024]{1,0:T(8,128)S(1)}, f32[1024,384]{1,0:T(8,128)S(1)}, bf16[1024,384]{1,0:T(8,128)(2,1)S(1)}, bf16[8,4,4,384,128]{4,3,2,1...) custom-call(bf16[16,192,128]{2,1,0:T(8,128)(2,1)S(1)} %get-tuple-ele, ...), custom_call_target="tpu_custom_call" | custom-call | tf_op jit(solution)/shard_map/assemble_factor_gather/pallas_call | solution.py:538
  217.7 17.1 %schur.1 = (bf16[1,6144,384]{2,1,0:T(8,128)(2,1)}, f32[64,1024]{1,0:T(8,128)}, f32[1,1024,384]{2,1,0:T(8,128)}) custom-call(bf16[8,16,384,128]{3,2,1,0:T(8,128)(2,1)} %bitcast.8, bf16[1024,384]{1,0:T(8,128)(2,1)S(1)} %get-tuple-element.26.s_ref, bf16[16,2,64,384]{3,2,1,0:T(8,128)(2,1)S(1)} %get-tuple-element.27.t0_ref, ...), custom_call_target="tpu_custom_call" | custom-call | tf_op jit(solution)/shard_map/schur/pallas_call | solution.py:596
Async XLA Ops:
  1.4 1.7 copy-start
  3.1 0.7 copy-start.3
  3.8 0.7 copy-start.4
  4.4 5.7 %copy-start.1 = (bf16[1,1024,384]{2,1,0:T(8,128)(2,1)S(1)}, bf16[1,1024,384]{2,1,0:T(8,128)(2,1)}, u32[]{:S(2)}) copy-start(bf16[1,1024,384]{2,1,0:T(8,128)(2,1)} %or_ref.1) | copy-start | bytes 2359300
  4.4 5.7 %copy-start.2 = (bf16[1,1024,64]{1,2,0:T(8,128)(2,1)S(1)}, bf16[1,1024,64]{1,2,0:T(8,128)(2,1)}, u32[]{:S(2)}) copy-start(bf16[1,1024,64]{1,2,0:T(8,128)(2,1)} %param.7) | copy-start | bytes 393220

commit v5 on v4

--- a/solution.py
+++ b/solution.py
@@ -308,10 +308,10 @@
 
 def main_kernel(
     ps1, a0, a1, a2, od_ref, or_ref, ints, floats,
-    ud_ref, ur_ref, s_ref, sg_ref, o0_ref, o1_ref, o2_ref,
-    pr1, ps2, pr2, b0, b1, b2, c0, c1, c2, dsnd, psnd, prcv,
-    w, m_ref, inv_ref, uh, ul, st, dall,
-    asend, arecv, dsend, drecv, ssend, srecv, lsem, ksem,
+    ud_ref, ur_ref, s_ref, sg_ref, acc_ref, end_ref,
+    pr1, ps2, pr2, b0, b1, b2, c0, c1, c2, dsnd, psnd,
+    w, m_ref, inv_ref, uh, ul, st, dall, tin, sv,
+    asend, arecv, dsend, drecv, ssend, srecv, lsem, ksem, vsem,
 ):
     f = lax.axis_index("front")
     g = lax.axis_index("grid")
@@ -334,15 +334,14 @@
 
     panel1 = swap(0, "grid", ps1, lambda me: pr1.at[me])
     panel2 = swap(1, "front", ps2, lambda me: pr2.at[pl.ds(3 * me, 3)])
-    pswap = swap(2, "grid", psnd, lambda me: prcv.at[pl.ds(64 * me, 64), :])
+    pswap = swap(2, "grid", psnd, lambda me: w.at[pl.ds(64 * me, 64), pl.ds(N, PC)])
 
     def trail1(s):
         dst = (b0, b1, b2)[s]
         return swap(3 + s, "grid", (a0, a1, a2)[s], lambda me: dst.at[pl.ds(2 * me, 2)])
 
     def trail2(s):
-        dst = (o0_ref, o1_ref, o2_ref)[s]
-        return swap(6 + s, "front", (c0, c1, c2)[s], lambda me: dst.at[me])
+        return swap(6 + s, "front", (c0, c1, c2)[s], lambda me: tin.at[3 * me + s])
 
     pl.semaphore_wait(barrier, 30)
     panel1.start()
@@ -446,6 +445,18 @@
             local(k).wait()
         c.start(n)
 
+    def load(n):
+        return pltpu.make_async_copy(sg_ref.at[pl.ds(2 * n, 2)], (sv, end_ref)[n % 2], vsem.at[n % 2])
+
+    def fetch(n):
+        for k in (2 * n, 2 * n + 1):
+            gs(k).wait_recv(2)
+        load(n).start()
+
+    def product(n, m):
+        lhs = jnp.concatenate([(sv, end_ref)[n % 2][k, m // 4, m % 4] for k in range(2)], 1)
+        return dg(lhs, s_ref[2 * NB * n : 2 * NB * (n + 1), :], 1, 0)
+
     def step(k, carry):
         r0 = pl.multiple_of(k * NB, NB)
         m_ref[:, :NB] = w[pl.ds(r0, NB), pl.ds(r0, NB)]
@@ -458,10 +469,15 @@
 
         factor_block(m_ref, inv_ref, hook)
 
+        @pl.when(k == N // NB - 1)
+        def _():
+            fetch(0)
+            fetch(1)
+
         @pl.when(k == 0)
         def _():
             pswap.wait_recv()
-            w[:, N:] = prcv[...] + or_ref[0].astype(F32)
+            w[:, N:] = w[:, N:] + or_ref[0].astype(F32)
 
         @pl.when(k == 2)
         def _():
@@ -501,7 +517,24 @@
 
     last = N // NB - 1
     lax.fori_loop(0, N // NB, step, 0)
+    load(0).wait()
+
+    def first(m, c):
+        acc_ref[pl.ds(pl.multiple_of(m * PC, PC), PC), :] = product(0, m)
+        return c
+
+    lax.fori_loop(0, 16, first, 0)
+    fetch(2)
     move(last, 1)
+    load(1).wait()
+
+    def second(m, c):
+        rows = pl.ds(pl.multiple_of(m * PC, PC), PC)
+        acc_ref[rows, :] = acc_ref[rows, :] + product(1, m)
+        return c
+
+    lax.fori_loop(0, 16, second, 0)
+    move(last, 2)
     blk = pl.multiple_of((g // 2) * NB, NB)
     col = 64 * g + lax.broadcasted_iota(jnp.int32, (64, NB), 0)
     for r in range(8):
@@ -509,28 +542,44 @@
         own = jnp.where(g % 2 == 1, own[64:], own[:64])
         row = r * NB + lax.broadcasted_iota(jnp.int32, (64, NB), 1)
         ud_ref[:, r * NB : (r + 1) * NB] = jnp.where(row <= col, own, 0.0)
-    move(last, 2)
     for s in range(3):
         trail1(s).wait_send()
         trail2(s).wait_send()
         trail2(s).wait_recv()
+    load(2).wait()
+
+    def third(m, c):
+        for i in range(3):
+            for v in range(2):
+                r = i * NB + v * 64
+                total = jnp.zeros((64, PC), F32)
+                for t in range(2):
+                    e = t * SLOTS + 8 + 3 * m + i
+                    total = total + tin[ints[UNIT + 2 * e + v], t].astype(F32) * floats[HAS + e]
+                rows = pl.ds(pl.multiple_of(m * PC + r, 64), 64)
+                acc_ref[rows, :] = total - acc_ref[rows, :]
+        rows = pl.ds(pl.multiple_of(m * PC, PC), PC)
+        acc_ref[rows, :] = acc_ref[rows, :] - product(2, m)
+        return c
+
+    lax.fori_loop(0, 16, third, 0)
     for e in (panel1, panel2, pswap):
         e.wait_send()
     gd.wait_send()
 
+    fetch(3)
+
     def finish(k, carry):
-        c = gs(k)
-        c.wait_recv(2)
-        c.wait_send()
+        gs(k).wait_send()
         return carry
 
     lax.fori_loop(0, N // NB, finish, 0)
+    load(3).wait()
 
 
 def main_call(ps1, a0, a1, a2, orig_diag, orig_rows, *tables):
     steps = N // NB
     hbm = pl.BlockSpec(memory_space=pl.ANY)
-    out = jax.ShapeDtypeStruct((16, 2, 64, PC), BF)
     panel = pltpu.VMEM((16, 192, NB), BF)
     send = pltpu.VMEM((16, 2, 64, PC), BF)
     recv = pltpu.VMEM((KIDS, 64, PC), BF)
@@ -542,16 +591,16 @@
             jax.ShapeDtypeStruct((N, PC), F32),
             jax.ShapeDtypeStruct((N, PC), BF),
             jax.ShapeDtypeStruct((steps, 4, 4, PC, NB), BF),
-            out, out, out,
+            jax.ShapeDtypeStruct((16 * PC, PC), F32),
+            jax.ShapeDtypeStruct((2, 4, 4, PC, NB), BF),
         ),
         in_specs=[vm(), vm(), vm(), vm(), vm(), vm(), sm(), sm()],
-        out_specs=(vm(), vm(), vm(), hbm, vm(), vm(), vm()),
+        out_specs=(vm(), vm(), vm(), hbm, vm(), vm()),
         scratch_shapes=[
             panel, pltpu.VMEM((16, 3, 64, NB), BF), pltpu.VMEM((48, 64, NB), BF),
             recv, recv, recv, send, send, send,
             pltpu.VMEM((64, PW), F32),
             pltpu.VMEM((16, 64, PC), F32),
-            pltpu.VMEM((N, PC), F32),
             pltpu.VMEM((N, WT), F32),
             pltpu.VMEM((NB, 2 * NB), F32),
             pltpu.VMEM((NB, NB), F32),
@@ -559,40 +608,32 @@
             pltpu.VMEM((NB, WT), BF),
             pltpu.VMEM((steps, PC, NB), BF),
             pltpu.VMEM((4, 4, 64, PW), F32),
+            pltpu.VMEM((48, 2, 64, PC), BF),
+            pltpu.VMEM((2, 4, 4, PC, NB), BF),
             sems((9, 16)), sems((9, 16)), sems((16,)), sems((16,)),
-            sems((steps, 16)), sems((steps, 16)), sems((steps,)), sems((9,)),
+            sems((steps, 16)), sems((steps, 16)), sems((steps,)), sems((9,)), sems((2,)),
         ],
         compiler_params=pltpu.CompilerParams(
-            vmem_limit_bytes=40 << 20, collective_id=0, has_side_effects=True
+            vmem_limit_bytes=65 << 19, collective_id=0, has_side_effects=True
         ),
         name="assemble_factor_gather",
     )(ps1, a0, a1, a2, orig_diag, orig_rows, *tables)
 
 
-def schur_kernel(
-    sg_ref, s_ref, t0_ref, t1_ref, t2_ref, ud_ref, ur_ref, slots, o_ref, udo_ref, uro_ref
-):
-    m = pl.program_id(0)
+def schur_kernel(end_ref, s_ref, acc_ref, ud_ref, ur_ref, o_ref, udo_ref, uro_ref):
     uro_ref[0] = ur_ref[...]
     udo_ref[...] = ud_ref[...]
-    lhs = jnp.concatenate([sg_ref[k, 0] for k in range(N // NB)], 1)
-    prod = dg(lhs, s_ref[...], 1, 0)
-    for i in range(3):
-        for v in range(2):
-            total = -prod[i * NB + v * 64 : i * NB + v * 64 + 64]
-            for t in range(2):
-                a = slots[FRONT + t * SLOTS + 8 + 3 * m + i]
-                u = 2 * jnp.maximum(a, 0) + v
-                s = u % 3
-                x = jnp.where(
-                    s == 0, t0_ref[u // 3, t], jnp.where(s == 1, t1_ref[u // 3, t], t2_ref[u // 3, t])
-                )
-                total = total + jnp.where(a >= 0, x.astype(F32), 0.0)
-            o_ref[0, i * NB + v * 64 : i * NB + v * 64 + 64, :] = total.astype(BF)
-
-
-def schur_call(sg, s, t0, t1, t2, ud, ur, ints):
-    steps = N // NB
+    m = pl.program_id(0)
+    for i in range(2):
+        b = 2 * m + i
+        lhs = jnp.concatenate([end_ref[k, b] for k in range(2)], 1)
+        rows = pl.ds(pl.multiple_of(b * PC, PC), PC)
+        o_ref[0, i * PC : (i + 1) * PC, :] = (
+            acc_ref[rows, :] - dg(lhs, s_ref[6 * NB :, :], 1, 0)
+        ).astype(BF)
+
+
+def schur_call(end, s, acc, ud, ur):
     return pl.pallas_call(
         schur_kernel,
         out_shape=(
@@ -600,30 +641,30 @@
             jax.ShapeDtypeStruct((64, N), F32),
             jax.ShapeDtypeStruct((1, N, PC), F32),
         ),
-        grid=(16,),
+        grid=(8,),
         in_specs=[
-            pl.BlockSpec((steps, 1, PC, NB), lambda m: (0, m, 0, 0)),
-            vm(), vm(), vm(), vm(),
-            pl.BlockSpec((64, NB), lambda m: (0, m // 2)),
-            pl.BlockSpec((64, PC), lambda m: (m, 0)),
-            sm(),
+            vm(),
+            vm(),
+            vm(),
+            pl.BlockSpec((64, NB), lambda m: (0, m)),
+            pl.BlockSpec((NB, PC), lambda m: (m, 0)),
         ],
         out_specs=(
-            pl.BlockSpec((1, PC, PC), lambda m: (0, m, 0)),
-            pl.BlockSpec((64, NB), lambda m: (0, m // 2)),
-            pl.BlockSpec((1, 64, PC), lambda m: (0, m, 0)),
+            pl.BlockSpec((1, 2 * PC, PC), lambda m: (0, m, 0)),
+            pl.BlockSpec((64, NB), lambda m: (0, m)),
+            pl.BlockSpec((1, NB, PC), lambda m: (0, m, 0)),
         ),
-        compiler_params=pltpu.CompilerParams(vmem_limit_bytes=46 << 20),
+        compiler_params=pltpu.CompilerParams(vmem_limit_bytes=20 << 20),
         name="schur",
-    )(sg.reshape(steps, 16, PC, NB), s, t0, t1, t2, ud, ur, ints)
+    )(end.reshape(2, 16, PC, NB), s, acc, ud, ur)
 
 
 def shards(child_blocks, orig_diag, orig_rows, child_map, child_parent, pivot_order):
     panel, a0, a1, a2, ints, floats = pack(child_blocks, child_map, child_parent, pivot_order)
-    upper_diag, upper_rows, s, sg, *trail = main_call(
+    upper_diag, upper_rows, s, _, acc, end = main_call(
         panel, a0, a1, a2, orig_diag[0].T, orig_rows, ints, floats
     )
-    schur, upper_diag, upper_rows = schur_call(sg, s, *trail, upper_diag, upper_rows, ints)
+    schur, upper_diag, upper_rows = schur_call(end, s, acc, upper_diag, upper_rows)
     return upper_diag.T[None], upper_rows, schur
 
 

time: 235 us -> 229 us (0.974)
  Pallas kernels: 230 us -> 225 us
    pallas_call x1, Pallas kernels: 17.1 us -> 5.24 us  [schur_call(): pl.pallas_call(schur_kernel, out_shape=(jax.ShapeDtypeStruct((1, 16 * PC,...]
    pallas_call x1, Pallas kernels: 208 us -> 214 us  [main_call(): pl.pallas_call(main_kernel, out_shape=(jax.ShapeDtypeStruct((64, N), F32)...]
where the time goes in v5:
time: 229 us
  Pallas kernels  225 us (98%)
  local copies, waits for them, and re-layouts  3.81 us (2%)
    pallas_call x1, Pallas kernels, main_call(): pl.pallas_call(main_kernel, out_shape=(jax.ShapeDtypeStruct((64, N), F32)...  214 us
    pallas_call x1, Pallas kernels, pack(): pl.pallas_call(pack_kernel, out_shape=(jax.ShapeDtypeStruct((16, 192, NB)...  5.69 us
    pallas_call x1, Pallas kernels, schur_call(): pl.pallas_call(schur_kernel, out_shape=(jax.ShapeDtypeStruct((1, 16 * PC,...  5.24 us

profile of v5, /device:TPU:2, one launch (start us, length us, event | category | flops | bytes accessed | tf_op | source)
XLA Modules:
  0.0 229.0 jit_solution(9178975566620309431)
XLA Ops:
  0.6 0.8 copy.9.map_ref
  1.4 0.0 copy-start
  1.4 1.7 copy-done
  3.1 0.0 copy-start.3
  3.1 0.7 copy-done.3
  3.8 0.0 copy-start.4
  3.8 0.7 copy-done.4
  4.4 0.0 copy-start.1
  4.4 0.0 copy-start.2
  4.4 5.7 %pack.1 = (bf16[16,192,128]{2,1,0:T(8,128)(2,1)S(1)}, bf16[16,2,64,384]{3,2,1,0:T(8,128)(2,1)S(1)}, bf16[16,2,64,384]{3,2,1,0:T(8,128)(2,1)S(1)}, bf16[16,2,64,3...) custom-call(bf16[2,192,3072]{2,1,0:T(8,128)(2,1)S(1)} %copy-done, s32[32,24]{1,0:T(8,128)S(1)} %copy.9.map_ref, ...), custom_call_target="tpu_custom_call" | custom-call | tf_op jit(solution)/shard_map/pack/pallas_call | solution.py:129
  10.1 0.0 copy-done.1
  10.1 0.0 copy-done.2
  10.2 213.6 %assemble_factor_gather.1 = (f32[64,1024]{1,0:T(8,128)S(1)}, f32[1024,384]{1,0:T(8,128)S(1)}, bf16[1024,384]{1,0:T(8,128)(2,1)S(1)}, bf16[8,4,4,384,128]{4,3,2,1...) custom-call(bf16[16,192,128]{2,1,0:T(8,128)(2,1)S(1)} %get-tuple-element.17.ps1, ...), custom_call_target="tpu_custom_call" | custom-call | tf_op jit(solution)/shard_map/assemble_factor_gather/pallas_call | solution.py:587
  223.8 5.2 %schur.1 = (bf16[1,6144,384]{2,1,0:T(8,128)(2,1)}, f32[64,1024]{1,0:T(8,128)}, f32[1,1024,384]{2,1,0:T(8,128)}) custom-call(bf16[2,16,384,128]{3,2,1,0:T(8,128)(2,1)S(1)} %bitcast.7, bf16[1024,384]{1,0:T(8,128)(2,1)S(1)} %get-tuple-element.24.s_ref, f32[6144,384]{1,0:T(8,128)S(1)} %get-tuple-element.25.acc_ref, f32[64,1024]{1,0:T(8,128)S(1)} %get-tuple-element.26.ud_ref, ...), custom_call_target="tpu_custom_call" | custom-call | tf_op jit(solution)/shard_map/schur/pallas_call | solution.py:637
Async XLA Ops:
  1.4 1.7 copy-start
  3.1 0.7 copy-start.3
  3.8 0.7 copy-start.4
  4.4 5.7 %copy-start.1 = (bf16[1,1024,384]{2,1,0:T(8,128)(2,1)S(1)}, bf16[1,1024,384]{2,1,0:T(8,128)(2,1)}, u32[]{:S(2)}) copy-start(bf16[1,1024,384]{2,1,0:T(8,128)(2,1)} %or_ref.1) | copy-start | bytes 2359300
  4.4 5.7 %copy-start.2 = (bf16[1,1024,64]{1,2,0:T(8,128)(2,1)S(1)}, bf16[1,1024,64]{1,2,0:T(8,128)(2,1)}, u32[]{:S(2)}) copy-start(bf16[1,1024,64]{1,2,0:T(8,128)(2,1)} %param.7) | copy-start | bytes 393220

commit v6 on v5

--- a/solution.py
+++ b/solution.py
@@ -150,7 +150,7 @@
     rid = lax.broadcasted_iota(jnp.int32, (8, 1), 0)
     rows = [m_ref[8 * r : 8 * r + 8, :] for r in range(16)]
     for q in range(16):
-        if q == 8:
+        if q == 5:
             hook()
         c0 = 8 * q
         rb = [jnp.broadcast_to(rows[q][s : s + 1, :], (8, 2 * NB)) for s in range(8)]
@@ -479,7 +479,7 @@
             pswap.wait_recv()
             w[:, N:] = w[:, N:] + or_ref[0].astype(F32)
 
-        @pl.when(k == 2)
+        @pl.when(k == 3)
         def _():
             sort_trail(2)
 

time: 229 us -> 228 us (level)
  no operation moved by 1% of the time
where the time goes in v6:
time: 228 us
  Pallas kernels  223 us (98%)
  local copies, waits for them, and re-layouts  3.81 us (2%)
    pallas_call x1, Pallas kernels, main_call(): pl.pallas_call(main_kernel, out_shape=(jax.ShapeDtypeStruct((64, N), F32)...  212 us
    pallas_call x1, Pallas kernels, pack(): pl.pallas_call(pack_kernel, out_shape=(jax.ShapeDtypeStruct((16, 192, NB)...  5.69 us
    pallas_call x1, Pallas kernels, schur_call(): pl.pallas_call(schur_kernel, out_shape=(jax.ShapeDtypeStruct((1, 16 * PC,...  5.24 us

profile of v6, /device:TPU:2, one launch (start us, length us, event | category | flops | bytes accessed | tf_op | source)
XLA Modules:
  0.0 227.7 jit_solution(9967345375317185141)
XLA Ops:
  0.6 0.8 copy.9.map_ref
  1.4 0.0 copy-start
  1.4 1.7 copy-done
  3.1 0.0 copy-start.3
  3.1 0.7 copy-done.3
  3.8 0.0 copy-start.4
  3.8 0.7 copy-done.4
  4.4 0.0 copy-start.1
  4.4 0.0 copy-start.2
  4.4 5.7 %pack.1 = (bf16[16,192,128]{2,1,0:T(8,128)(2,1)S(1)}, bf16[16,2,64,384]{3,2,1,0:T(8,128)(2,1)S(1)}, bf16[16,2,64,384]{3,2,1,0:T(8,128)(2,1)S(1)}, bf16[16,2,64,3...) custom-call(bf16[2,192,3072]{2,1,0:T(8,128)(2,1)S(1)} %copy-done, s32[32,24]{1,0:T(8,128)S(1)} %copy.9.map_ref, ...), custom_call_target="tpu_custom_call" | custom-call | tf_op jit(solution)/shard_map/pack/pallas_call | solution.py:129
  10.1 0.0 copy-done.1
  10.1 0.0 copy-done.2
  10.2 212.3 %assemble_factor_gather.1 = (f32[64,1024]{1,0:T(8,128)S(1)}, f32[1024,384]{1,0:T(8,128)S(1)}, bf16[1024,384]{1,0:T(8,128)(2,1)S(1)}, bf16[8,4,4,384,128]{4,3,2,1...) custom-call(bf16[16,192,128]{2,1,0:T(8,128)(2,1)S(1)} %get-tuple-element.17.ps1, ...), custom_call_target="tpu_custom_call" | custom-call | tf_op jit(solution)/shard_map/assemble_factor_gather/pallas_call | solution.py:587
  222.4 5.2 %schur.1 = (bf16[1,6144,384]{2,1,0:T(8,128)(2,1)}, f32[64,1024]{1,0:T(8,128)}, f32[1,1024,384]{2,1,0:T(8,128)}) custom-call(bf16[2,16,384,128]{3,2,1,0:T(8,128)(2,1)S(1)} %bitcast.7, bf16[1024,384]{1,0:T(8,128)(2,1)S(1)} %get-tuple-element.24.s_ref, f32[6144,384]{1,0:T(8,128)S(1)} %get-tuple-element.25.acc_ref, f32[64,1024]{1,0:T(8,128)S(1)} %get-tuple-element.26.ud_ref, ...), custom_call_target="tpu_custom_call" | custom-call | tf_op jit(solution)/shard_map/schur/pallas_call | solution.py:637
Async XLA Ops:
  1.4 1.7 copy-start
  3.1 0.7 copy-start.3
  3.8 0.7 copy-start.4
  4.4 5.7 %copy-start.1 = (bf16[1,1024,384]{2,1,0:T(8,128)(2,1)S(1)}, bf16[1,1024,384]{2,1,0:T(8,128)(2,1)}, u32[]{:S(2)}) copy-start(bf16[1,1024,384]{2,1,0:T(8,128)(2,1)} %or_ref.1) | copy-start | bytes 2359300
  4.4 5.7 %copy-start.2 = (bf16[1,1024,64]{1,2,0:T(8,128)(2,1)S(1)}, bf16[1,1024,64]{1,2,0:T(8,128)(2,1)}, u32[]{:S(2)}) copy-start(bf16[1,1024,64]{1,2,0:T(8,128)(2,1)} %param.7) | copy-start | bytes 393220
